TPU v7x, 256 devices: a whole 4x4x8 slice. The times are simulated.
256 devices in a mesh: rows: 256 (over z, x, y, core).
Axes of the slice: x: 4, y: 4, z: 8, core: 2. Of those that a mesh axis runs over, the one named last changes fastest.
Arguments:
- matrix: float32 [1048576, 128], P('rows')
- flips: int32 [1048576], P('rows'), may hold values from 0 to 1
- picks: int32 [16384], P('rows'), may hold values from 0 to 4095, as said below
Outputs:
- sketch: float32 [16384, 128], P('rows')
- factor: float32 [128, 128], replicated
Inputs may be any that keep to these rules, and one draw needn't show every extreme that they name: `picks`: each index lies within its owner's slab; repeated indices may occur.
All inputs are finite; a program needn't handle non-finite values.
Results may differ from a plain program's by a relative error of at most 0.00014.
Values sent between devices are 32-bit elements; how exact they have to be, the bound alone decides.
A program may use at most 64 MiB of HBM per device.

v0:
```python
import math

import jax
import jax.numpy as jnp
from jax import lax
from jax.sharding import PartitionSpec as P


def swapped(value, axis, stride):
    mask = 2**stride
    pairs = [(source, source ^ mask) for source in range(lax.axis_size(axis))]
    return lax.ppermute(value, axis, pairs)


def hadamard(order):
    index = lax.iota(jnp.int32, order)
    parity_sum = jnp.zeros((order, order), jnp.int32)
    for digit in range(order.bit_length()):
        parity_sum = parity_sum + (index[:, None] >> digit & 1) * (index[None, :] >> digit & 1)
    return (1 - 2 * (parity_sum % 2)).astype(jnp.float32)


def slab_transform(values):
    height = values.shape[0]
    width = values.shape[1]
    inner = 128
    outer = height // inner
    blocks = values.reshape(outer, inner, width)
    mixed = jnp.einsum(
        "ij,ajc->aic",
        hadamard(inner),
        blocks,
        precision=lax.Precision.HIGHEST,
        preferred_element_type=jnp.float32,
    )
    mixed = jnp.einsum(
        "ab,bic->aic",
        hadamard(outer),
        mixed,
        precision=lax.Precision.HIGHEST,
        preferred_element_type=jnp.float32,
    )
    return mixed.reshape(height, width)


def shards(matrix, flips, picks):
    devices = lax.axis_size("rows")
    digits = devices.bit_length() - 1
    myself = lax.axis_index("rows")
    height = matrix.shape[0]
    per_device = picks.shape[0]
    signs = (1 - 2 * flips).astype(jnp.float32)
    local = slab_transform(matrix * signs[:, None])
    scale = 1.0 / math.sqrt(height * devices)
    order_list = list(range(digits))
    values = local
    for digit in order_list:
        partner = swapped(values, "rows", digit)
        upper = myself >> digit & 1 == 1
        values = jnp.where(upper, partner - values, values + partner)
    sketch = jnp.take(values, picks, axis=0) * scale
    partial_gram = jnp.dot(
        sketch.T, sketch, preferred_element_type=jnp.float32, precision=lax.Precision.HIGHEST
    )
    gram = lax.psum(partial_gram, "rows") / (per_device * devices)
    factor = jnp.linalg.cholesky(gram)
    return (sketch, factor)


def solution(mesh):
    placed = (P("rows", None), P("rows"), P("rows"))
    return jax.shard_map(
        shards, mesh=mesh, in_specs=placed, out_specs=(P("rows", None), P()), check_vma=False
    )
```

profile of v0, /device:TPU:1, one launch (start us, length us, event | category | flops | bytes accessed | tf_op | source)
XLA Modules:
  0.0 735.6 jit_solution(15239661016108178442)
XLA Ops:
  7.2 0.0 all-reduce.2.cloned.1.call-start
  7.3 0.7 subtract_convert_fusion
  8.0 2.2 broadcast_multiply_fusion
  10.2 5.0 fusion.7
  15.2 2.4 copy.10
  17.6 1.9 fusion
  19.5 1.2 copy.7
  20.7 0.0 copy-start.2
  20.7 3.3 collective-permute-start
  24.0 0.0 copy-done.2
  24.0 3.9 collective-permute-done
  28.0 2.4 add_select_fusion.7
  30.4 0.0 copy-start.1
  30.4 0.1 collective-permute-start.1
  30.5 1.2 copy-done.1
  31.7 45.7 %collective-permute-done.1 = f32[4096,128]{1,0:T(8,128)} collective-permute-done((f32[4096,128]{1,0:T(8,128)S(1)}, f32[4096,128]{1,0:T(8,128)}, u32[]{:S(2)}, u32[]{:S(2)}) %collective-permute-start.1) | collective-permute-done | bytes 2097184 | tf_op jit(solution)/shard_map/ppermute | solution.py:12
  77.4 2.4 add_select_fusion.6
  79.9 1.3 collective-permute-start.2
  81.2 46.4 %collective-permute-done.2 = f32[4096,128]{1,0:T(8,128)} collective-permute-done((f32[4096,128]{1,0:T(8,128)S(1)}, f32[4096,128]{1,0:T(8,128)}, u32[]{:S(2)}, u32[]{:S(2)}) %collective-permute-start.2) | collective-permute-done | bytes 2097184 | tf_op jit(solution)/shard_map/ppermute | solution.py:12
  127.5 3.1 add_select_fusion.5
  130.7 0.0 collective-permute-start.3
  130.7 45.4 %collective-permute-done.3 = f32[4096,128]{1,0:T(8,128)} collective-permute-done((f32[4096,128]{1,0:T(8,128)}, f32[4096,128]{1,0:T(8,128)}, u32[]{:S(2)}, u32[]{:S(2)}) %collective-permute-start.3) | collective-permute-done | bytes 2097184 | tf_op jit(solution)/shard_map/ppermute | solution.py:12
  176.1 2.4 add_select_fusion.4
  178.5 1.1 collective-permute-start.4
  179.7 44.8 %collective-permute-done.4 = f32[4096,128]{1,0:T(8,128)} collective-permute-done((f32[4096,128]{1,0:T(8,128)S(1)}, f32[4096,128]{1,0:T(8,128)}, u32[]{:S(2)}, u32[]{:S(2)}) %collective-permute-start.4) | collective-permute-done | bytes 2097184 | tf_op jit(solution)/shard_map/ppermute | solution.py:12
  224.5 3.1 add_select_fusion.3
  227.6 0.0 collective-permute-start.5
  227.6 43.7 %collective-permute-done.5 = f32[4096,128]{1,0:T(8,128)} collective-permute-done((f32[4096,128]{1,0:T(8,128)}, f32[4096,128]{1,0:T(8,128)}, u32[]{:S(2)}, u32[]{:S(2)}) %collective-permute-start.5) | collective-permute-done | bytes 2097184 | tf_op jit(solution)/shard_map/ppermute | solution.py:12
  271.3 2.4 add_select_fusion.2
  273.8 0.0 copy-start
  273.8 1.7 collective-permute-start.6
  275.5 0.0 copy-done
  275.5 0.0 copy-start.4
  275.5 91.6 %collective-permute-done.6 = f32[4096,128]{1,0:T(8,128)} collective-permute-done((f32[4096,128]{1,0:T(8,128)S(1)}, f32[4096,128]{1,0:T(8,128)}, u32[]{:S(2)}, u32[]{:S(2)}) %collective-permute-start.6) | collective-permute-done | bytes 2097184 | tf_op jit(solution)/shard_map/ppermute | solution.py:12
  367.1 2.4 add_select_fusion.1
  369.5 5.1 collective-permute-start.7
  374.7 0.0 copy-done.4
  374.7 90.6 %collective-permute-done.7 = f32[4096,128]{1,0:T(8,128)} collective-permute-done((f32[4096,128]{1,0:T(8,128)S(1)}, f32[4096,128]{1,0:T(8,128)}, u32[]{:S(2)}, u32[]{:S(2)}) %collective-permute-start.7) | collective-permute-done | bytes 2097184 | tf_op jit(solution)/shard_map/ppermute | solution.py:12
  465.3 3.1 add_select_fusion
  468.4 2.2 gather_fusion
  470.6 0.1 select_multiply_fusion
  470.7 0.0 copy-start.3
  470.7 0.9 fusion.62
  471.6 0.0 all-reduce.2.cloned.1.call-update
  471.7 241.6 %all-reduce.2.cloned.1.call-done = f32[128,128]{0,1:T(8,128)} async-done(((f32[128,128]{0,1:T(8,128)}), f32[128,128]{0,1:T(8,128)}) %all-reduce.2.cloned.1.call-update) | async-done | bytes 65552 | tf_op jit(solution)/shard_map/psum | solution.py:65
  713.2 0.8 broadcast_multiply_fusion.1
  714.1 0.1 copy.9
  714.2 0.9 fusion.9
  715.0 11.7 %cholesky.18 = f32[128,128]{1,0:T(8,128)S(1)} custom-call(f32[128,128]{1,0:T(8,128)S(1)} %fusion.9), custom_call_target="Cholesky" | custom-call | tf_op jit(solution)/shard_map/jit(cholesky)/cholesky | solution.py:66
  726.8 0.7 compare_reduce_fusion
  727.5 1.3 select_select_fusion
  728.7 0.0 copy-done.3
  (11 shorter events, 0.1 us)
Async XLA Ops:
  7.2 706.1 %all-reduce.2.cloned.1.call-start = ((), (), s32[]{:S(2)}) async-start(), calls=%async_computation | async-start | bytes 131072 | tf_op jit(solution)/shard_map/psum | solution.py:65
  20.7 3.3 copy-start.2
  20.7 7.2 collective-permute-start
  30.4 1.3 copy-start.1
  30.4 47.0 %collective-permute-start.1 = (f32[4096,128]{1,0:T(8,128)S(1)}, f32[4096,128]{1,0:T(8,128)}, u32[]{:S(2)}, u32[]{:S(2)}) collective-permute-start(f32[4096,128]{1,0:T(8,128)S(1)} %add_select_fusion.7), channel_id=1, source_target_pairs={{0,2},{1,3},{2,0},{3,1},{4,6},{5,7},{6,4},{7,5},{8,10},{9,11},{10,... | collective-permute-start | bytes 6291464 | tf_op jit(solution)/shard_map/ppermute | solution.py:12
  79.9 47.7 %collective-permute-start.2 = (f32[4096,128]{1,0:T(8,128)S(1)}, f32[4096,128]{1,0:T(8,128)}, u32[]{:S(2)}, u32[]{:S(2)}) collective-permute-start(f32[4096,128]{1,0:T(8,128)S(1)} %add_select_fusion.6), channel_id=1, source_target_pairs={{0,4},{1,5},{2,6},{3,7},{4,0},{5,1},{6,2},{7,3},{8,12},{9,13},{10,... | collective-permute-start | bytes 6291464 | tf_op jit(solution)/shard_map/ppermute | solution.py:12
  130.7 45.4 %collective-permute-start.3 = (f32[4096,128]{1,0:T(8,128)}, f32[4096,128]{1,0:T(8,128)}, u32[]{:S(2)}, u32[]{:S(2)}) collective-permute-start(f32[4096,128]{1,0:T(8,128)} %add_select_fusion.5), channel_id=1, source_target_pairs={{0,8},{1,9},{2,10},{3,11},{4,12},{5,13},{6,14},{7,15},{8,0},{9,1},... | collective-permute-start | bytes 6291464 | tf_op jit(solution)/shard_map/ppermute | solution.py:12
  178.5 45.9 %collective-permute-start.4 = (f32[4096,128]{1,0:T(8,128)S(1)}, f32[4096,128]{1,0:T(8,128)}, u32[]{:S(2)}, u32[]{:S(2)}) collective-permute-start(f32[4096,128]{1,0:T(8,128)S(1)} %add_select_fusion.4), channel_id=1, source_target_pairs={{0,16},{1,17},{2,18},{3,19},{4,20},{5,21},{6,22},{7,23},{8,24},{9,... | collective-permute-start | bytes 6291464 | tf_op jit(solution)/shard_map/ppermute | solution.py:12
  227.6 43.7 %collective-permute-start.5 = (f32[4096,128]{1,0:T(8,128)}, f32[4096,128]{1,0:T(8,128)}, u32[]{:S(2)}, u32[]{:S(2)}) collective-permute-start(f32[4096,128]{1,0:T(8,128)} %add_select_fusion.3), channel_id=1, source_target_pairs={{0,32},{1,33},{2,34},{3,35},{4,36},{5,37},{6,38},{7,39},{8,40},{9,... | collective-permute-start | bytes 6291464 | tf_op jit(solution)/shard_map/ppermute | solution.py:12
  273.8 1.7 copy-start
  273.8 93.3 %collective-permute-start.6 = (f32[4096,128]{1,0:T(8,128)S(1)}, f32[4096,128]{1,0:T(8,128)}, u32[]{:S(2)}, u32[]{:S(2)}) collective-permute-start(f32[4096,128]{1,0:T(8,128)S(1)} %add_select_fusion.2), channel_id=1, source_target_pairs={{0,64},{1,65},{2,66},{3,67},{4,68},{5,69},{6,70},{7,71},{8,72},{9,... | collective-permute-start | bytes 6291464 | tf_op jit(solution)/shard_map/ppermute | solution.py:12
  275.5 99.2 %copy-start.4 = (s32[64]{0:T(128)S(1)}, s32[64]{0:T(128)}, u32[]{:S(2)}) copy-start(s32[64]{0:T(128)} %param.5) | copy-start | bytes 772
  369.5 95.8 %collective-permute-start.7 = (f32[4096,128]{1,0:T(8,128)S(1)}, f32[4096,128]{1,0:T(8,128)}, u32[]{:S(2)}, u32[]{:S(2)}) collective-permute-start(f32[4096,128]{1,0:T(8,128)S(1)} %add_select_fusion.1), channel_id=1, source_target_pairs={{0,128},{1,129},{2,130},{3,131},{4,132},{5,133},{6,134},{7,135},{8... | collective-permute-start | bytes 6291464 | tf_op jit(solution)/shard_map/ppermute | solution.py:12
  470.7 258.0 %copy-start.3 = (f32[64,128]{1,0:T(8,128)}, f32[64,128]{1,0:T(8,128)S(1)}, u32[]{:S(2)}) copy-start(f32[64,128]{1,0:T(8,128)S(1)} %select_multiply_fusion) | copy-start | bytes 98308
Sparse Core Ops, SparseCore 0:
  471.8 241.4 all-reduce.1
where the time goes:
time: 736 us
  waiting for transfers between devices  654 us (89%)
  other arithmetic  40.1 us (5%)
  between operations  14.2 us (2%)
  starting transfers between devices  12.7 us (2%)
  matrix products  7.84 us (1%)
    ppermute x8, waiting for transfers between devices, swapped(): return lax.ppermute(value, axis, pairs)  412 us
    psum x1, waiting for transfers between devices, shards(): gram = lax.psum(partial_gram, 'rows') / (per_device * devices)  242 us
    select_n x8, other arithmetic, shards(): values = jnp.where(upper, partner - values, values + partner)  21.6 us
  transfers between devices with their start and end apart: 9, of which 9 were waited for; matrix products, arithmetic and copies ran while one was open for 0% of the time, Pallas kernels for 0%

commit v1 on v0

v1 whole, which is shorter than its diff:
```python
import jax
import jax.numpy as jnp
from jax import lax
from jax.experimental import pallas as pl
from jax.experimental.pallas import tpu as pltpu
from jax.sharding import PartitionSpec as P

MESH = pl.DeviceIdType.MESH
F32 = jnp.float32
BF16 = jnp.bfloat16

RING = 4
DEPTH = 8
ROWS = 4096
COLS = 128
PER = 64
BLOCK = 256
BLOCKS = ROWS // BLOCK
CHUNKS = 8
CHUNK = ROWS // CHUNKS
PART_A = RING * DEPTH * PER // 2
PART_B = DEPTH * PER // 2
PIECE = COLS // RING


def parity_sign(left, right):
    both = left & right
    both = (both ^ (both >> 1) ^ (both >> 2)) & 1
    return (1 - 2 * both).astype(F32)


def hadamard_block():
    row = lax.broadcasted_iota(jnp.int32, (BLOCK, BLOCK), 0)
    col = lax.broadcasted_iota(jnp.int32, (BLOCK, BLOCK), 1)
    both = row & col
    both = both ^ (both >> 4)
    both = both ^ (both >> 2)
    both = both ^ (both >> 1)
    return (1 - 2 * (both & 1)).astype(F32).astype(BF16)


def kernel(
    mat, flips, picks, sketch, gram,
    own, par, flips_par, had, mixed, picked, picked_s,
    out_a, opp_a, from_left_a, from_right_a, tot_a,
    out_b, opp_b, from_left_b, from_right_b, tot_b,
    got_z, part_g, got_ga, piece_b, piece_z, full_g, other_g,
    load_sem, core_send, core_recv, flip_sems, pick_send, pick_recv, pick_local,
    a_send, a_recv, b_send, b_recv, z_send, z_recv, g_send, g_recv,
):
    me = lax.axis_index("rows")
    core = lax.rem(me, 2)
    ypos = lax.rem(lax.div(me, 2), RING)
    xpos = lax.rem(lax.div(me, 2 * RING), RING)
    z = lax.div(me, 2 * RING * RING)
    a = ypos + core * (xpos - ypos)
    b = xpos + core * (ypos - xpos)
    step_a = 2 + core * (2 * RING - 2)
    step_b = 2 * RING - core * (2 * RING - 2)
    partner = me + 1 - 2 * core

    def turn(position, by, size):
        return lax.rem(position + by, size)

    def peer_a(by):
        return me + (turn(a, by, RING) - a) * step_a

    def peer_b(by):
        return me + (turn(b, by, RING) - b) * step_b

    def peer_z(by):
        return me + (turn(z, by, DEPTH) - z) * (2 * RING * RING)

    def remote(src, dst, send, recv, device):
        return pltpu.make_async_remote_copy(
            src_ref=src, dst_ref=dst, send_sem=send, recv_sem=recv,
            device_id=(device,), device_id_type=MESH,
        )

    loads = []
    for k in range(CHUNKS):
        rows = pl.ds(k * CHUNK, CHUNK)
        load = pltpu.make_async_copy(mat.at[rows], own.at[rows], load_sem.at[k])
        load.start()
        loads.append(load)

    barrier = pltpu.get_barrier_semaphore()
    peers = [partner] + [peer_a(k) for k in range(1, RING)] + [peer_b(k) for k in range(1, RING)]
    peers += [peer_z(k) for k in range(1, DEPTH)]
    for device in peers:
        pl.semaphore_signal(barrier, inc=1, device_id=(device,), device_id_type=MESH)

    had[...] = hadamard_block()

    def transformed(block, values, flip_ref, sign):
        negative = jnp.concatenate([flip_ref[pl.ds(2 * block, 1), :], flip_ref[pl.ds(2 * block + 1, 1), :]], axis=1)
        signs = ((1 - 2 * negative).astype(F32) * sign).astype(BF16)
        high = values.astype(BF16)
        low = (values - high.astype(F32)).astype(BF16)
        both = jnp.concatenate([high, low], axis=1)
        product = jnp.dot(had[...] * signs, both, preferred_element_type=F32)
        return product[:, :COLS] + product[:, COLS:]

    own_sign = parity_sign(core, core)
    par_sign = jnp.float32(1.0)
    for k in range(CHUNKS):
        loads[k].wait()
        for j in range(CHUNK // BLOCK):
            block = k * (CHUNK // BLOCK) + j
            rows = pl.ds(block * BLOCK, BLOCK)
            mixed[rows, :] = transformed(block, own[rows, :], flips, own_sign)

    pl.semaphore_wait(barrier, len(peers))

    flip_copy = remote(flips, flips_par, flip_sems.at[0], flip_sems.at[1], partner)
    flip_copy.start()
    core_copies = []
    for k in range(CHUNKS):
        rows = pl.ds(k * CHUNK, CHUNK)
        copy = remote(mat.at[rows], par.at[rows], core_send.at[k], core_recv.at[k], partner)
        copy.start()
        core_copies.append(copy)

    slot = (z * RING + b) * RING + a
    keep = pltpu.make_async_copy(picks, picked.at[slot], pick_local.at[0])
    keep.start()
    picks_a = []
    for k in range(1, RING):
        copy = remote(picks, picked.at[slot], pick_send.at[k - 1], pick_recv.at[k - 1], peer_a(k))
        copy.start()
        picks_a.append(copy)

    def fold(k):
        for j in range(CHUNK // BLOCK):
            block = k * (CHUNK // BLOCK) + j
            rows = pl.ds(block * BLOCK, BLOCK)
            mixed[rows, :] += transformed(block, par[rows, :], flips_par, par_sign)

    flip_copy.wait()
    keep.wait()
    for k in range(2):
        core_copies[k].wait()
        fold(k)
    for copy in picks_a:
        copy.wait()
    picks_b = []
    line = pl.ds((z * RING + b) * RING, RING)
    for k in range(1, RING):
        copy = remote(picked.at[line], picked.at[line], pick_send.at[k + 2], pick_recv.at[k + 2], peer_b(k))
        copy.start()
        picks_b.append(copy)
    for k in range(2, 5):
        core_copies[k].wait()
        fold(k)
    for copy in picks_b:
        copy.wait()
    picks_z = []
    plane = pl.ds(z * RING * RING, RING * RING)
    for k in range(1, DEPTH):
        copy = remote(picked.at[plane], picked.at[plane], pick_send.at[k + 5], pick_recv.at[k + 5], peer_z(k))
        copy.start()
        picks_z.append(copy)
    for k in range(5, CHUNKS):
        core_copies[k].wait()
        fold(k)

    def butterfly(i, carry):
        values = [mixed[pl.ds(j * BLOCK + pl.multiple_of(i * 8, 8), 8), :] for j in range(BLOCKS)]
        span = 1
        while span < BLOCKS:
            after = list(values)
            for j in range(BLOCKS):
                if not j & span:
                    after[j] = values[j] + values[j + span]
                    after[j + span] = values[j] - values[j + span]
            values = after
            span *= 2
        for j in range(BLOCKS):
            mixed[pl.ds(j * BLOCK + pl.multiple_of(i * 8, 8), 8), :] = values[j]
        return carry

    lax.fori_loop(0, BLOCK // 8, butterfly, 0)

    for copy in picks_z:
        copy.wait()
    to_scalar = pltpu.make_async_copy(picked, picked_s, pick_local.at[1])
    to_scalar.start()
    to_scalar.wait()

    def gather(dst, base, dest, half):
        sign = parity_sign(dest, a)

        def body(q, carry):
            b_to = half * (RING // 2) + lax.div(q, DEPTH)
            z_to = lax.rem(q, DEPTH)
            place = (z_to * RING + b_to) * RING + dest
            for g in range(PER // 16):
                rows = [mixed[pl.ds(picked_s[place, 0, g * 16 + s], 1), :] for s in range(16)]
                for s in range(16):
                    dst[pl.ds(base + q * PER + g * 16 + s, 1), :] = rows[s] * sign
            return carry

        lax.fori_loop(0, RING // 2 * DEPTH, body, 0)

    right, left = peer_a(1), peer_a(RING - 1)
    at_right, at_left, at_opp = turn(a, 1, RING), turn(a, 3, RING), turn(a, 2, RING)

    def send_a(k, dst, device):
        copy = remote(out_a.at[k], dst, a_send.at[k], a_recv.at[k], device)
        copy.start()
        return copy

    gather(out_a.at[0], 0, at_opp, 0)
    c0 = send_a(0, opp_a.at[0], right)
    gather(out_a.at[1], 0, at_opp, 1)
    c1 = send_a(1, opp_a.at[1], left)
    gather(out_a.at[2], 0, at_right, 1)
    c2 = send_a(2, from_left_a.at[1], right)
    gather(out_a.at[3], 0, at_left, 0)
    c3 = send_a(3, from_right_a.at[0], left)
    gather(out_a.at[4], 0, at_right, 0)
    c0.wait_recv()
    out_a[4] += opp_a[0]
    c4 = send_a(4, from_left_a.at[0], right)
    gather(out_a.at[5], 0, at_left, 1)
    c1.wait_recv()
    out_a[5] += opp_a[1]
    c5 = send_a(5, from_right_a.at[1], left)
    gather(tot_a, 0, a, 0)
    gather(tot_a, PART_A, a, 1)
    c2.wait_recv()
    c3.wait_recv()

    def total_a(half):
        for j in range(RING // 2):
            b_to = half * (RING // 2) + j
            rows = pl.ds(b_to * 2 * PART_B, 2 * PART_B)
            inner = pl.ds(j * 2 * PART_B, 2 * PART_B)
            summed = tot_a[rows, :] + from_left_a[half, inner, :] + from_right_a[half, inner, :]
            tot_a[rows, :] = summed * parity_sign(jnp.int32(b_to), b)

    c4.wait_recv()
    total_a(0)
    c5.wait_recv()
    total_a(1)

    b_right, b_left, b_opp = turn(b, 1, RING), turn(b, 3, RING), turn(b, 2, RING)
    right_b, left_b = peer_b(1), peer_b(RING - 1)

    def rows_b(dest, half):
        return pl.ds(pl.multiple_of(dest * (2 * PART_B) + half * PART_B, 8), PART_B)

    def send_b(k, src, dst, device):
        copy = remote(src, dst, b_send.at[k], b_recv.at[k], device)
        copy.start()
        return copy

    d0 = send_b(0, tot_a.at[rows_b(b_opp, 0)], opp_b.at[0], right_b)
    d1 = send_b(1, tot_a.at[rows_b(b_opp, 1)], opp_b.at[1], left_b)
    d2 = send_b(2, tot_a.at[rows_b(b_right, 1)], from_left_b.at[1], right_b)
    d3 = send_b(3, tot_a.at[rows_b(b_left, 0)], from_right_b.at[0], left_b)
    d0.wait_recv()
    out_b[0] = tot_a[rows_b(b_right, 0), :] + opp_b[0]
    d4 = send_b(4, out_b.at[0], from_left_b.at[0], right_b)
    d1.wait_recv()
    out_b[1] = tot_a[rows_b(b_left, 1), :] + opp_b[1]
    d5 = send_b(5, out_b.at[1], from_right_b.at[1], left_b)
    d2.wait_recv()
    d3.wait_recv()

    def total_b(half):
        for j in range(DEPTH // 2):
            z_to = half * (DEPTH // 2) + j
            inner = pl.ds(j * PER, PER)
            own_rows = pl.ds(pl.multiple_of(b * (2 * PART_B) + z_to * PER, 8), PER)
            summed = tot_a[own_rows, :] + from_left_b[half, inner, :] + from_right_b[half, inner, :]
            tot_b[z_to] = summed * parity_sign(jnp.int32(z_to), z)

    d4.wait_recv()
    total_b(0)
    d5.wait_recv()
    total_b(1)

    z_copies = []
    for k in (4, 3, 5, 2, 6, 1, 7):
        copy = remote(tot_b.at[turn(z, k, DEPTH)], got_z.at[k - 1], z_send.at[k - 1], z_recv.at[k - 1], peer_z(k))
        copy.start()
        z_copies.append(copy)
    for copy in z_copies:
        copy.wait_recv()
    rows = tot_b[z]
    for k in range(DEPTH - 1):
        rows = rows + got_z[k]
    rows = rows * (1.0 / 1024.0)
    sketch[...] = rows

    part_g[...] = lax.dot_general(
        rows, rows, (((0,), (0,)), ((), ())), precision=lax.Precision.HIGHEST, preferred_element_type=F32
    )

    def send_g(k, src, dst, device):
        copy = remote(src, dst, g_send.at[k], g_recv.at[k], device)
        copy.start()
        return copy

    def piece(position):
        return pl.ds(pl.multiple_of(position * PIECE, PIECE), PIECE)

    copies = [send_g(k - 1, part_g.at[piece(turn(a, k, RING))], got_ga.at[k - 1], peer_a(k)) for k in range(1, RING)]
    for copy in copies:
        copy.wait_recv()
    piece_b[b] = part_g[piece(a), :] + got_ga[0] + got_ga[1] + got_ga[2]
    pending = copies
    copies = [send_g(k + 2, piece_b.at[b], piece_b.at[b], peer_b(k)) for k in range(1, RING)]
    for copy in copies:
        copy.wait_recv()
    piece_z[z] = piece_b[0] + piece_b[1] + piece_b[2] + piece_b[3]
    pending = pending + copies
    copies = [send_g(k + 5, piece_z.at[z], piece_z.at[z], peer_z(k)) for k in (4, 3, 5, 2, 6, 1, 7)]
    for copy in copies:
        copy.wait_recv()
    total = piece_z[0]
    for k in range(1, DEPTH):
        total = total + piece_z[k]
    full_g[piece(a), :] = total
    pending = pending + copies
    copies = [send_g(k + 12, full_g.at[piece(a)], full_g.at[piece(a)], peer_a(k)) for k in range(1, RING)]
    for copy in copies:
        copy.wait_recv()
    pending = pending + copies
    last = send_g(16, full_g, other_g, partner)
    last.wait_recv()
    gram[...] = (full_g[...] + other_g[...]) * (1.0 / (PER * 2 * RING * RING * DEPTH))
    pending = pending + [last]

    for copy in [c0, c1, c2, c3, c4, c5, d0, d1, d2, d3, d4, d5] + z_copies + pending:
        copy.wait_send()


def shards(matrix, flips, picks):
    vmem = pl.BlockSpec(memory_space=pltpu.VMEM)
    half_a = (PART_A, COLS)
    half_b = (PART_B, COLS)
    dma = pltpu.SemaphoreType.DMA
    sketch, gram = pl.pallas_call(
        kernel,
        name="blendenpik",
        out_shape=(
            jax.ShapeDtypeStruct((PER, COLS), F32),
            jax.ShapeDtypeStruct((COLS, COLS), F32),
        ),
        in_specs=[pl.BlockSpec(memory_space=pl.ANY), vmem, vmem],
        out_specs=(vmem, vmem),
        scratch_shapes=[
            pltpu.VMEM((ROWS, COLS), F32),
            pltpu.VMEM((ROWS, COLS), F32),
            pltpu.VMEM((ROWS // COLS, COLS), jnp.int32),
            pltpu.VMEM((BLOCK, BLOCK), BF16),
            pltpu.VMEM((ROWS, COLS), F32),
            pltpu.VMEM((RING * RING * DEPTH, 1, PER), jnp.int32),
            pltpu.SMEM((RING * RING * DEPTH, 1, PER), jnp.int32),
            pltpu.VMEM((6, *half_a), F32),
            pltpu.VMEM((2, *half_a), F32),
            pltpu.VMEM((2, *half_a), F32),
            pltpu.VMEM((2, *half_a), F32),
            pltpu.VMEM((2 * PART_A, COLS), F32),
            pltpu.VMEM((2, *half_b), F32),
            pltpu.VMEM((2, *half_b), F32),
            pltpu.VMEM((2, *half_b), F32),
            pltpu.VMEM((2, *half_b), F32),
            pltpu.VMEM((DEPTH, PER, COLS), F32),
            pltpu.VMEM((DEPTH - 1, PER, COLS), F32),
            pltpu.VMEM((COLS, COLS), F32),
            pltpu.VMEM((RING - 1, PIECE, COLS), F32),
            pltpu.VMEM((RING, PIECE, COLS), F32),
            pltpu.VMEM((DEPTH, PIECE, COLS), F32),
            pltpu.VMEM((COLS, COLS), F32),
            pltpu.VMEM((COLS, COLS), F32),
            dma((CHUNKS,)),
            dma((CHUNKS,)),
            dma((CHUNKS,)),
            dma((2,)),
            dma((13,)),
            dma((13,)),
            dma((2,)),
            dma((6,)),
            dma((6,)),
            dma((6,)),
            dma((6,)),
            dma((7,)),
            dma((7,)),
            dma((17,)),
            dma((17,)),
        ],
        compiler_params=pltpu.CompilerParams(
            collective_id=0, has_side_effects=True, vmem_limit_bytes=48 * 1024 * 1024
        ),
    )(matrix, flips.reshape(ROWS // COLS, COLS), picks.reshape(1, PER))
    factor = lax.linalg.cholesky(gram, symmetrize_input=False)
    return (sketch, factor)


def solution(mesh):
    placed = (P("rows", None), P("rows"), P("rows"))
    return jax.shard_map(
        shards, mesh=mesh, in_specs=placed, out_specs=(P("rows", None), P()), check_vma=False
    )
```

time: 736 us -> 98.7 us (0.13)
  waiting for transfers between devices: 654 us -> 0 us
  Pallas kernels: 0 us -> 80.6 us
  other arithmetic: 40.1 us -> 13.7 us
  between operations: 14.2 us -> 0.65 us
  starting transfers between devices: 12.7 us -> 0 us
  matrix products: 7.84 us -> 0 us
    ppermute x8 -> x0, waiting for transfers between devices: 412 us -> none  [swapped(): return lax.ppermute(value, axis, pairs)]
    psum x1 -> x0, waiting for transfers between devices: 242 us -> none  [shards(): gram = lax.psum(partial_gram, 'rows') / (per_device * devices)]
    pallas_call x0 -> x1, Pallas kernels: none -> 80.6 us  [shards(): pl.pallas_call(kernel, name='blendenpik', out_shape=(jax.ShapeDtypeStruct...]
    select_n x10 -> x1, other arithmetic: 22.9 us -> 1.29 us  [shards(): factor = lax.linalg.cholesky(gram, symmetrize_input=False)]
    ppermute x8 -> x0, starting transfers between devices: 12.6 us -> none  [swapped(): return lax.ppermute(value, axis, pairs)]
    dot_general x3 -> x0, matrix products: 7.84 us -> none  [the longest x1 5 us: slab_transform(): jnp.einsum('ij,ajc->aic', hadamard(inner), blocks, precision=lax.Precisio...]
  transfers between devices with their start and end apart: 9 -> 0, of which waited for: 9 -> 0; matrix products, arithmetic and copies ran while one was open for 0% -> 0% of each run, Pallas kernels for 0% -> 0%
where the time goes in v1:
time: 98.7 us; the launch traced here: 98.5 us
  Pallas kernels  80.6 us (82%)
  other arithmetic  13.7 us (14%)
  local copies, waits for them, and re-layouts  3.57 us (4%)
    pallas_call x1, Pallas kernels, shards(): pl.pallas_call(kernel, name='blendenpik', out_shape=(jax.ShapeDtypeStruct...  80.6 us
    another operation x3, other arithmetic, shards(): factor = lax.linalg.cholesky(gram, symmetrize_input=False)  12.4 us
    unnamed x7, local copies, waits for them, and re-layouts  3.57 us

profile of v1, /device:TPU:1, one launch (start us, length us, event | category | flops | bytes accessed | tf_op | source)
XLA Modules:
  0.0 98.5 jit_solution(9302650528350895087)
XLA Ops:
  0.6 0.0 copy-start
  0.6 1.6 %copy-done = f32[4096,128]{1,0:T(8,128)S(1)} copy-done((f32[4096,128]{1,0:T(8,128)S(1)}, f32[4096,128]{1,0:T(8,128)}, u32[]{:S(2)}) %copy-start) | copy-done | bytes 2097176
  2.2 0.0 copy-start.1
  2.2 0.7 copy-done.1
  2.9 0.0 copy-start.2
  2.9 0.7 copy-done.2
  3.6 80.6 %blendenpik.1 = (f32[64,128]{1,0:T(8,128)S(1)}, f32[128,128]{1,0:T(8,128)S(1)}) custom-call(f32[4096,128]{1,0:T(8,128)S(1)} %copy-done, s32[32,128]{1,0:T(8,128)S(1)} %bitcast.2, s32[1,64]{1,0:T(1,128)S(1)} %bitcast.3), custom_call_target="tpu_custom_call" | custom-call | tf_op jit(solution)/shard_map/blendenpik/pallas_call | solution.py:345
  84.2 11.7 %cholesky.18 = f32[128,128]{1,0:T(8,128)S(1)} custom-call(f32[128,128]{1,0:T(8,128)S(1)} %get-tuple-element.5), custom_call_target="Cholesky" | custom-call | tf_op jit(solution)/shard_map/cholesky | solution.py:399
  96.0 0.6 compare_reduce_fusion
  96.6 1.3 %select_select_fusion = f32[128,128]{1,0:T(8,128)} fusion(f32[128,128]{1,0:T(8,128)S(1)} %cholesky.18, pred[]{:T(512)} %compare_reduce_fusion), kind=kLoop, calls=%fused_computation | loop fusion | flops 49152 | bytes 131073 | tf_op jit(solution)/shard_map/select_n | solution.py:399
  97.9 0.6 copy.6
  (1 shorter events, 0.0 us)
Async XLA Ops:
  0.6 1.6 %copy-start = (f32[4096,128]{1,0:T(8,128)S(1)}, f32[4096,128]{1,0:T(8,128)}, u32[]{:S(2)}) copy-start(f32[4096,128]{1,0:T(8,128)} %mat.1) | copy-start | bytes 6291460
  2.2 0.7 copy-start.1
  2.9 0.7 copy-start.2

commit v2 on v1

--- a/solution.py
+++ b/solution.py
@@ -21,6 +21,7 @@
 PART_A = RING * DEPTH * PER // 2
 PART_B = DEPTH * PER // 2
 PIECE = COLS // RING
+PANEL = 16
 
 
 def parity_sign(left, right):
@@ -40,12 +41,12 @@
 
 
 def kernel(
-    mat, flips, picks, sketch, gram,
-    own, par, flips_par, had, mixed, picked, picked_s,
+    mat, flips_in, picks, sketch, gram,
+    own, par, flips, flips_par, had, mixed, picked, picked_s,
     out_a, opp_a, from_left_a, from_right_a, tot_a,
     out_b, opp_b, from_left_b, from_right_b, tot_b,
     got_z, part_g, got_ga, piece_b, piece_z, full_g, other_g,
-    load_sem, core_send, core_recv, flip_sems, pick_send, pick_recv, pick_local,
+    load_sem, flip_load, go, ready, core_send, core_recv, flip_sems, pick_send, pick_recv, pick_local, scalar_sem,
     a_send, a_recv, b_send, b_recv, z_send, z_recv, g_send, g_recv,
 ):
     me = lax.axis_index("rows")
@@ -77,18 +78,72 @@
             device_id=(device,), device_id_type=MESH,
         )
 
+    barrier = pltpu.get_barrier_semaphore()
+    plane = [peer_a(k) for k in range(1, RING)] + [peer_b(k) for k in range(1, RING)]
+    column = [peer_z(k) for k in range(1, DEPTH)]
+
+    def signal(semaphore, device):
+        pl.semaphore_signal(semaphore, inc=1, device_id=(device,), device_id_type=MESH)
+
+    @pl.when(core == 0)
+    def _():
+        for device in plane:
+            signal(barrier, device)
+
+    @pl.when(core == 1)
+    def _():
+        signal(barrier, partner)
+
     loads = []
     for k in range(CHUNKS):
         rows = pl.ds(k * CHUNK, CHUNK)
         load = pltpu.make_async_copy(mat.at[rows], own.at[rows], load_sem.at[k])
         load.start()
         loads.append(load)
-
-    barrier = pltpu.get_barrier_semaphore()
-    peers = [partner] + [peer_a(k) for k in range(1, RING)] + [peer_b(k) for k in range(1, RING)]
-    peers += [peer_z(k) for k in range(1, DEPTH)]
-    for device in peers:
-        pl.semaphore_signal(barrier, inc=1, device_id=(device,), device_id_type=MESH)
+    flip_in = pltpu.make_async_copy(flips_in, flips, flip_load.at[0])
+    flip_in.start()
+    slot = (z * RING + b) * RING + a
+    keep = pltpu.make_async_copy(picks, picked.at[slot], pick_local.at[0])
+    keep.start()
+
+    @pl.when(core == 0)
+    def _():
+        pl.semaphore_wait(barrier, 1 + len(plane))
+        signal(go.at[0], partner)
+
+    @pl.when(core == 1)
+    def _():
+        pl.semaphore_wait(go.at[0], 1)
+        for device in column:
+            signal(barrier, device)
+
+    flip_copy = remote(flips_in, flips_par, flip_sems.at[0], flip_sems.at[1], partner)
+    flip_copy.start()
+    core_copies = []
+    for k in range(CHUNKS):
+        rows = pl.ds(k * CHUNK, CHUNK)
+        copy = remote(mat.at[rows], par.at[rows], core_send.at[k], core_recv.at[k], partner)
+        copy.start()
+        core_copies.append(copy)
+
+    picks_a = [
+        remote(picks, picked.at[slot], pick_send.at[k - 1], pick_recv.at[k - 1], peer_a(k)) for k in range(1, RING)
+    ]
+
+    @pl.when(core == 0)
+    def _():
+        for copy in picks_a:
+            copy.start()
+        for device in plane:
+            signal(ready, device)
+        pl.semaphore_wait(ready, len(plane))
+        signal(go.at[1], partner)
+
+    @pl.when(core == 1)
+    def _():
+        pl.semaphore_wait(go.at[1], 1)
+        for copy in picks_a:
+            copy.start()
 
     had[...] = hadamard_block()
 
@@ -103,6 +158,7 @@
 
     own_sign = parity_sign(core, core)
     par_sign = jnp.float32(1.0)
+    flip_in.wait()
     for k in range(CHUNKS):
         loads[k].wait()
         for j in range(CHUNK // BLOCK):
@@ -110,37 +166,14 @@
             rows = pl.ds(block * BLOCK, BLOCK)
             mixed[rows, :] = transformed(block, own[rows, :], flips, own_sign)
 
-    pl.semaphore_wait(barrier, len(peers))
-
-    flip_copy = remote(flips, flips_par, flip_sems.at[0], flip_sems.at[1], partner)
-    flip_copy.start()
-    core_copies = []
-    for k in range(CHUNKS):
-        rows = pl.ds(k * CHUNK, CHUNK)
-        copy = remote(mat.at[rows], par.at[rows], core_send.at[k], core_recv.at[k], partner)
-        copy.start()
-        core_copies.append(copy)
-
-    slot = (z * RING + b) * RING + a
-    keep = pltpu.make_async_copy(picks, picked.at[slot], pick_local.at[0])
-    keep.start()
-    picks_a = []
-    for k in range(1, RING):
-        copy = remote(picks, picked.at[slot], pick_send.at[k - 1], pick_recv.at[k - 1], peer_a(k))
-        copy.start()
-        picks_a.append(copy)
-
     def fold(k):
+        core_copies[k].wait()
         for j in range(CHUNK // BLOCK):
             block = k * (CHUNK // BLOCK) + j
             rows = pl.ds(block * BLOCK, BLOCK)
             mixed[rows, :] += transformed(block, par[rows, :], flips_par, par_sign)
 
-    flip_copy.wait()
     keep.wait()
-    for k in range(2):
-        core_copies[k].wait()
-        fold(k)
     for copy in picks_a:
         copy.wait()
     picks_b = []
@@ -149,19 +182,28 @@
         copy = remote(picked.at[line], picked.at[line], pick_send.at[k + 2], pick_recv.at[k + 2], peer_b(k))
         copy.start()
         picks_b.append(copy)
-    for k in range(2, 5):
-        core_copies[k].wait()
+
+    @pl.when(core == 1)
+    def _():
+        pl.semaphore_wait(barrier, len(column))
+        signal(go.at[2], partner)
+
+    @pl.when(core == 0)
+    def _():
+        pl.semaphore_wait(go.at[2], 1)
+
+    flip_copy.wait()
+    for k in range(2):
         fold(k)
     for copy in picks_b:
         copy.wait()
     picks_z = []
-    plane = pl.ds(z * RING * RING, RING * RING)
-    for k in range(1, DEPTH):
-        copy = remote(picked.at[plane], picked.at[plane], pick_send.at[k + 5], pick_recv.at[k + 5], peer_z(k))
-        copy.start()
-        picks_z.append(copy)
-    for k in range(5, CHUNKS):
-        core_copies[k].wait()
+    layer = pl.ds(z * RING * RING, RING * RING)
+    for k in (4, 3, 5, 2, 6, 1, 7):
+        copy = remote(picked.at[layer], picked.at[layer], pick_send.at[k + 5], pick_recv.at[k + 5], peer_z(k))
+        copy.start()
+        picks_z.append((k, copy))
+    for k in range(2, CHUNKS):
         fold(k)
 
     def butterfly(i, carry):
@@ -181,11 +223,20 @@
 
     lax.fori_loop(0, BLOCK // 8, butterfly, 0)
 
-    for copy in picks_z:
+    scalar_copies = []
+
+    def to_scalar(by):
+        part = pl.ds(turn(z, by, DEPTH) * (RING * RING), RING * RING)
+        copy = pltpu.make_async_copy(picked.at[part], picked_s.at[part], scalar_sem.at[by])
+        copy.start()
+        scalar_copies.append(copy)
+
+    to_scalar(0)
+    for k, copy in reversed(picks_z):
         copy.wait()
-    to_scalar = pltpu.make_async_copy(picked, picked_s, pick_local.at[1])
-    to_scalar.start()
-    to_scalar.wait()
+        to_scalar(DEPTH - k)
+    for copy in scalar_copies:
+        copy.wait()
 
     def gather(dst, base, dest, half):
         sign = parity_sign(dest, a)
@@ -337,6 +388,38 @@
         copy.wait_send()
 
 
+def cholesky_kernel(gram, factor, work, upper):
+    work[...] = gram[...]
+    row = lax.broadcasted_iota(jnp.int32, (PANEL, COLS), 0)
+    lane = lax.broadcasted_iota(jnp.int32, (PANEL, COLS), 1)
+    for base in range(0, COLS, PANEL):
+        panel = work[pl.ds(base, PANEL), :]
+        columns = [jnp.broadcast_to(panel[:, base + k : base + k + 1], (PANEL, COLS)) for k in range(PANEL)]
+        pivots = jnp.ones((PANEL, COLS), F32)
+        for j in range(PANEL):
+            pivot = columns[j][j : j + 1, :]
+            pivots = jnp.where(row == j, columns[j], pivots)
+            factors = jnp.where(row > j, columns[j] * (1.0 / pivot), 0.0)
+            for k in range(j + 1, PANEL):
+                columns[k] = columns[k] - factors * columns[k][j : j + 1, :]
+            panel = panel - factors * panel[j : j + 1, :]
+        root = lax.rsqrt(pivots)
+        root = root * (1.5 - 0.5 * pivots * root * root)
+        scaled = jnp.where(lane >= base + row, panel * root, 0.0)
+        upper[pl.ds(base, PANEL), :] = scaled
+        if base + PANEL < COLS:
+            high = scaled.astype(BF16)
+            rest = scaled - high.astype(F32)
+            mid = rest.astype(BF16)
+            low = (rest - mid.astype(F32)).astype(BF16)
+            first = jnp.concatenate([high, high, mid, high, low, mid], axis=0)
+            second = jnp.concatenate([high, mid, high, low, high, mid], axis=0)
+            update = lax.dot_general(first, second, (((0,), (0,)), ((), ())), preferred_element_type=F32)
+            after = base + PANEL
+            work[pl.ds(after, COLS - after), :] -= update[after:, :]
+    factor[...] = upper[...].T
+
+
 def shards(matrix, flips, picks):
     vmem = pl.BlockSpec(memory_space=pltpu.VMEM)
     half_a = (PART_A, COLS)
@@ -349,11 +432,12 @@
             jax.ShapeDtypeStruct((PER, COLS), F32),
             jax.ShapeDtypeStruct((COLS, COLS), F32),
         ),
-        in_specs=[pl.BlockSpec(memory_space=pl.ANY), vmem, vmem],
+        in_specs=[pl.BlockSpec(memory_space=pltpu.HBM)] * 3,
         out_specs=(vmem, vmem),
         scratch_shapes=[
             pltpu.VMEM((ROWS, COLS), F32),
             pltpu.VMEM((ROWS, COLS), F32),
+            pltpu.VMEM((ROWS // COLS, COLS), jnp.int32),
             pltpu.VMEM((ROWS // COLS, COLS), jnp.int32),
             pltpu.VMEM((BLOCK, BLOCK), BF16),
             pltpu.VMEM((ROWS, COLS), F32),
@@ -377,12 +461,16 @@
             pltpu.VMEM((COLS, COLS), F32),
             pltpu.VMEM((COLS, COLS), F32),
             dma((CHUNKS,)),
+            dma((1,)),
+            pltpu.SemaphoreType.REGULAR((3,)),
+            pltpu.SemaphoreType.REGULAR,
             dma((CHUNKS,)),
             dma((CHUNKS,)),
             dma((2,)),
             dma((13,)),
             dma((13,)),
-            dma((2,)),
+            dma((1,)),
+            dma((DEPTH,)),
             dma((6,)),
             dma((6,)),
             dma((6,)),
@@ -396,7 +484,14 @@
             collective_id=0, has_side_effects=True, vmem_limit_bytes=48 * 1024 * 1024
         ),
     )(matrix, flips.reshape(ROWS // COLS, COLS), picks.reshape(1, PER))
-    factor = lax.linalg.cholesky(gram, symmetrize_input=False)
+    factor = pl.pallas_call(
+        cholesky_kernel,
+        name="factor",
+        out_shape=jax.ShapeDtypeStruct((COLS, COLS), F32),
+        in_specs=[vmem],
+        out_specs=vmem,
+        scratch_shapes=[pltpu.VMEM((COLS, COLS), F32)] * 2,
+    )(gram)
     return (sketch, factor)
 
 

time: 98.7 us -> 87 us (0.88)
  other arithmetic: 13.7 us -> 0 us
  Pallas kernels: 80.6 us -> 82 us
    another operation x3 -> x0, other arithmetic: 12.4 us -> none  [shards(): factor = lax.linalg.cholesky(gram, symmetrize_input=False)]
    pallas_call x0 -> x1, Pallas kernels: none -> 5 us  [shards(): pl.pallas_call(cholesky_kernel, name='factor', out_shape=jax.ShapeDtypeSt...]
    pallas_call x1, Pallas kernels: 80.6 us -> 77 us  [shards(): pl.pallas_call(kernel, name='blendenpik', out_shape=(jax.ShapeDtypeStruct...]
    select_n x1 -> x0, other arithmetic: 1.29 us -> none  [shards(): factor = lax.linalg.cholesky(gram, symmetrize_input=False)]
    unnamed x7 -> x9, local copies, waits for them, and re-layouts: 3.57 us -> 4.18 us
where the time goes in v2:
time: 87 us; the launch traced here: 86.8 us
  Pallas kernels  82 us (94%)
  local copies, waits for them, and re-layouts  4.18 us (5%)
    pallas_call x1, Pallas kernels, shards(): pl.pallas_call(kernel, name='blendenpik', out_shape=(jax.ShapeDtypeStruct...  77 us
    pallas_call x1, Pallas kernels, shards(): pl.pallas_call(cholesky_kernel, name='factor', out_shape=jax.ShapeDtypeSt...  5 us
    unnamed x9, local copies, waits for them, and re-layouts  4.18 us

profile of v2, /device:TPU:1, one launch (start us, length us, event | category | flops | bytes accessed | tf_op | source)
XLA Modules:
  0.0 86.8 jit_solution(5755729228364892942)
XLA Ops:
  0.6 0.0 copy-start
  0.6 1.6 %copy-done = f32[4096,128]{1,0:T(8,128)S(1)} copy-done((f32[4096,128]{1,0:T(8,128)S(1)}, f32[4096,128]{1,0:T(8,128)}, u32[]{:S(2)}) %copy-start) | copy-done | bytes 2097176
  2.2 0.0 copy-start.2
  2.2 0.7 copy-done.2
  2.9 0.0 copy-start.3
  2.9 0.7 copy-done.3
  3.6 77.0 %blendenpik.1 = (f32[64,128]{1,0:T(8,128)S(1)}, f32[128,128]{1,0:T(8,128)S(1)}) custom-call(f32[4096,128]{1,0:T(8,128)S(1)} %copy-done, s32[32,128]{1,0:T(8,128)S(1)} %bitcast.2, s32[1,64]{1,0:T(1,128)S(1)} %bitcast.3), custom_call_target="tpu_custom_call" | custom-call | tf_op jit(solution)/shard_map/blendenpik/pallas_call | solution.py:428
  80.6 0.0 copy-start.1
  80.6 0.6 copy-done.1
  81.2 5.0 %factor.1 = f32[128,128]{1,0:T(8,128)} custom-call(f32[128,128]{1,0:T(8,128)} %copy-done.1), custom_call_target="tpu_custom_call" | custom-call | tf_op jit(solution)/shard_map/factor/pallas_call | solution.py:487
  86.2 0.6 copy.6
Async XLA Ops:
  0.6 1.6 %copy-start = (f32[4096,128]{1,0:T(8,128)S(1)}, f32[4096,128]{1,0:T(8,128)}, u32[]{:S(2)}) copy-start(f32[4096,128]{1,0:T(8,128)} %mat.1) | copy-start | bytes 6291460
  2.2 0.7 copy-start.2
  2.9 0.7 copy-start.3
  80.6 0.6 copy-start.1

commit v3 on v2

--- a/solution.py
+++ b/solution.py
@@ -18,8 +18,7 @@
 BLOCKS = ROWS // BLOCK
 CHUNKS = 8
 CHUNK = ROWS // CHUNKS
-PART_A = RING * DEPTH * PER // 2
-PART_B = DEPTH * PER // 2
+LAG = 2
 PIECE = COLS // RING
 PANEL = 16
 
@@ -106,45 +105,6 @@
     keep = pltpu.make_async_copy(picks, picked.at[slot], pick_local.at[0])
     keep.start()
 
-    @pl.when(core == 0)
-    def _():
-        pl.semaphore_wait(barrier, 1 + len(plane))
-        signal(go.at[0], partner)
-
-    @pl.when(core == 1)
-    def _():
-        pl.semaphore_wait(go.at[0], 1)
-        for device in column:
-            signal(barrier, device)
-
-    flip_copy = remote(flips_in, flips_par, flip_sems.at[0], flip_sems.at[1], partner)
-    flip_copy.start()
-    core_copies = []
-    for k in range(CHUNKS):
-        rows = pl.ds(k * CHUNK, CHUNK)
-        copy = remote(mat.at[rows], par.at[rows], core_send.at[k], core_recv.at[k], partner)
-        copy.start()
-        core_copies.append(copy)
-
-    picks_a = [
-        remote(picks, picked.at[slot], pick_send.at[k - 1], pick_recv.at[k - 1], peer_a(k)) for k in range(1, RING)
-    ]
-
-    @pl.when(core == 0)
-    def _():
-        for copy in picks_a:
-            copy.start()
-        for device in plane:
-            signal(ready, device)
-        pl.semaphore_wait(ready, len(plane))
-        signal(go.at[1], partner)
-
-    @pl.when(core == 1)
-    def _():
-        pl.semaphore_wait(go.at[1], 1)
-        for copy in picks_a:
-            copy.start()
-
     had[...] = hadamard_block()
 
     def transformed(block, values, flip_ref, sign):
@@ -166,6 +126,45 @@
             rows = pl.ds(block * BLOCK, BLOCK)
             mixed[rows, :] = transformed(block, own[rows, :], flips, own_sign)
 
+    @pl.when(core == 0)
+    def _():
+        pl.semaphore_wait(barrier, 1 + len(plane))
+        signal(go.at[0], partner)
+
+    @pl.when(core == 1)
+    def _():
+        pl.semaphore_wait(go.at[0], 1)
+        for device in column:
+            signal(barrier, device)
+
+    flip_copy = remote(flips_in, flips_par, flip_sems.at[0], flip_sems.at[1], partner)
+    flip_copy.start()
+    core_copies = []
+    for k in range(CHUNKS):
+        rows = pl.ds(k * CHUNK, CHUNK)
+        copy = remote(mat.at[rows], par.at[rows], core_send.at[k], core_recv.at[k], partner)
+        copy.start()
+        core_copies.append(copy)
+
+    picks_a = [
+        remote(picks, picked.at[slot], pick_send.at[k - 1], pick_recv.at[k - 1], peer_a(k)) for k in range(1, RING)
+    ]
+
+    @pl.when(core == 0)
+    def _():
+        for copy in picks_a:
+            copy.start()
+        for device in plane:
+            signal(ready, device)
+        pl.semaphore_wait(ready, len(plane))
+        signal(go.at[1], partner)
+
+    @pl.when(core == 1)
+    def _():
+        pl.semaphore_wait(go.at[1], 1)
+        for copy in picks_a:
+            copy.start()
+
     def fold(k):
         core_copies[k].wait()
         for j in range(CHUNK // BLOCK):
@@ -197,12 +196,16 @@
         fold(k)
     for copy in picks_b:
         copy.wait()
-    picks_z = []
     layer = pl.ds(z * RING * RING, RING * RING)
-    for k in (4, 3, 5, 2, 6, 1, 7):
-        copy = remote(picked.at[layer], picked.at[layer], pick_send.at[k + 5], pick_recv.at[k + 5], peer_z(k))
-        copy.start()
-        picks_z.append((k, copy))
+
+    def picks_z(by):
+        return remote(
+            picked.at[layer], picked.at[layer], pick_send.at[6 + by], pick_recv.at[6 + by],
+            peer_z(DEPTH - by),
+        )
+
+    for by in (1, 7, 2, 6, 3, 5, 4):
+        picks_z(by).start()
     for k in range(2, CHUNKS):
         fold(k)
 
@@ -223,125 +226,132 @@
 
     lax.fori_loop(0, BLOCK // 8, butterfly, 0)
 
-    scalar_copies = []
-
-    def to_scalar(by):
-        part = pl.ds(turn(z, by, DEPTH) * (RING * RING), RING * RING)
-        copy = pltpu.make_async_copy(picked.at[part], picked_s.at[part], scalar_sem.at[by])
-        copy.start()
-        scalar_copies.append(copy)
-
-    to_scalar(0)
-    for k, copy in reversed(picks_z):
-        copy.wait()
-        to_scalar(DEPTH - k)
-    for copy in scalar_copies:
-        copy.wait()
-
-    def gather(dst, base, dest, half):
+    def offset(j):
+        pair = lax.div(j, 2)
+        return (pair + 1 + lax.rem(j, 2) * (6 - 2 * pair)) * (1 - lax.div(j, DEPTH - 1))
+
+    def picks_to_scalar(j):
+        part = pl.ds(turn(z, offset(j), DEPTH) * (RING * RING), RING * RING)
+        return pltpu.make_async_copy(picked.at[part], picked_s.at[part], scalar_sem.at[j])
+
+    def fetch(j):
+        @pl.when(j < DEPTH - 1)
+        def _():
+            by = offset(j)
+            remote(
+                picked.at[layer], picked.at[layer], pick_send.at[6 + by], pick_recv.at[6 + by], peer_z(by)
+            ).wait_recv()
+
+        picks_to_scalar(j).start()
+
+    def gather(j, k, dest, half):
         sign = parity_sign(dest, a)
+        z_to = turn(z, offset(j), DEPTH)
 
         def body(q, carry):
-            b_to = half * (RING // 2) + lax.div(q, DEPTH)
-            z_to = lax.rem(q, DEPTH)
-            place = (z_to * RING + b_to) * RING + dest
+            place = (z_to * RING + half * (RING // 2) + q) * RING + dest
             for g in range(PER // 16):
                 rows = [mixed[pl.ds(picked_s[place, 0, g * 16 + s], 1), :] for s in range(16)]
                 for s in range(16):
-                    dst[pl.ds(base + q * PER + g * 16 + s, 1), :] = rows[s] * sign
+                    out_a[j, k, pl.ds(q * PER + g * 16 + s, 1), :] = rows[s] * sign
             return carry
 
-        lax.fori_loop(0, RING // 2 * DEPTH, body, 0)
+        lax.fori_loop(0, RING // 2, body, 0)
 
     right, left = peer_a(1), peer_a(RING - 1)
     at_right, at_left, at_opp = turn(a, 1, RING), turn(a, 3, RING), turn(a, 2, RING)
-
-    def send_a(k, dst, device):
-        copy = remote(out_a.at[k], dst, a_send.at[k], a_recv.at[k], device)
-        copy.start()
-        return copy
-
-    gather(out_a.at[0], 0, at_opp, 0)
-    c0 = send_a(0, opp_a.at[0], right)
-    gather(out_a.at[1], 0, at_opp, 1)
-    c1 = send_a(1, opp_a.at[1], left)
-    gather(out_a.at[2], 0, at_right, 1)
-    c2 = send_a(2, from_left_a.at[1], right)
-    gather(out_a.at[3], 0, at_left, 0)
-    c3 = send_a(3, from_right_a.at[0], left)
-    gather(out_a.at[4], 0, at_right, 0)
-    c0.wait_recv()
-    out_a[4] += opp_a[0]
-    c4 = send_a(4, from_left_a.at[0], right)
-    gather(out_a.at[5], 0, at_left, 1)
-    c1.wait_recv()
-    out_a[5] += opp_a[1]
-    c5 = send_a(5, from_right_a.at[1], left)
-    gather(tot_a, 0, a, 0)
-    gather(tot_a, PART_A, a, 1)
-    c2.wait_recv()
-    c3.wait_recv()
-
-    def total_a(half):
-        for j in range(RING // 2):
-            b_to = half * (RING // 2) + j
-            rows = pl.ds(b_to * 2 * PART_B, 2 * PART_B)
-            inner = pl.ds(j * 2 * PART_B, 2 * PART_B)
-            summed = tot_a[rows, :] + from_left_a[half, inner, :] + from_right_a[half, inner, :]
-            tot_a[rows, :] = summed * parity_sign(jnp.int32(b_to), b)
-
-    c4.wait_recv()
-    total_a(0)
-    c5.wait_recv()
-    total_a(1)
-
     b_right, b_left, b_opp = turn(b, 1, RING), turn(b, 3, RING), turn(b, 2, RING)
     right_b, left_b = peer_b(1), peer_b(RING - 1)
 
-    def rows_b(dest, half):
-        return pl.ds(pl.multiple_of(dest * (2 * PART_B) + half * PART_B, 8), PART_B)
-
-    def send_b(k, src, dst, device):
-        copy = remote(src, dst, b_send.at[k], b_recv.at[k], device)
-        copy.start()
-        return copy
-
-    d0 = send_b(0, tot_a.at[rows_b(b_opp, 0)], opp_b.at[0], right_b)
-    d1 = send_b(1, tot_a.at[rows_b(b_opp, 1)], opp_b.at[1], left_b)
-    d2 = send_b(2, tot_a.at[rows_b(b_right, 1)], from_left_b.at[1], right_b)
-    d3 = send_b(3, tot_a.at[rows_b(b_left, 0)], from_right_b.at[0], left_b)
-    d0.wait_recv()
-    out_b[0] = tot_a[rows_b(b_right, 0), :] + opp_b[0]
-    d4 = send_b(4, out_b.at[0], from_left_b.at[0], right_b)
-    d1.wait_recv()
-    out_b[1] = tot_a[rows_b(b_left, 1), :] + opp_b[1]
-    d5 = send_b(5, out_b.at[1], from_right_b.at[1], left_b)
-    d2.wait_recv()
-    d3.wait_recv()
-
-    def total_b(half):
-        for j in range(DEPTH // 2):
-            z_to = half * (DEPTH // 2) + j
-            inner = pl.ds(j * PER, PER)
-            own_rows = pl.ds(pl.multiple_of(b * (2 * PART_B) + z_to * PER, 8), PER)
-            summed = tot_a[own_rows, :] + from_left_b[half, inner, :] + from_right_b[half, inner, :]
-            tot_b[z_to] = summed * parity_sign(jnp.int32(z_to), z)
-
-    d4.wait_recv()
-    total_b(0)
-    d5.wait_recv()
-    total_b(1)
-
-    z_copies = []
-    for k in (4, 3, 5, 2, 6, 1, 7):
-        copy = remote(tot_b.at[turn(z, k, DEPTH)], got_z.at[k - 1], z_send.at[k - 1], z_recv.at[k - 1], peer_z(k))
-        copy.start()
-        z_copies.append(copy)
-    for copy in z_copies:
-        copy.wait_recv()
-    rows = tot_b[z]
-    for k in range(DEPTH - 1):
-        rows = rows + got_z[k]
+    def copy_a(j, k):
+        dst = (
+            opp_a.at[j, 0], opp_a.at[j, 1], from_left_a.at[j, 1],
+            from_right_a.at[j, 0], from_left_a.at[j, 0], from_right_a.at[j, 1],
+        )[k]
+        return remote(out_a.at[j, k], dst, a_send.at[j, k], a_recv.at[j, k], left if k % 2 else right)
+
+    low, high = pl.ds(0, PER // 2), pl.ds(PER // 2, PER // 2)
+
+    def copy_b(j, k):
+        src, dst = (
+            (tot_a.at[j, b_opp, low], opp_b.at[j, 0]),
+            (tot_a.at[j, b_opp, high], opp_b.at[j, 1]),
+            (tot_a.at[j, b_right, high], from_left_b.at[j, 1]),
+            (tot_a.at[j, b_left, low], from_right_b.at[j, 0]),
+            (out_b.at[j, 0], from_left_b.at[j, 0]),
+            (out_b.at[j, 1], from_right_b.at[j, 1]),
+        )[k]
+        return remote(src, dst, b_send.at[j, k], b_recv.at[j, k], left_b if k % 2 else right_b)
+
+    def copy_z(j):
+        return remote(tot_b.at[j], got_z.at[j], z_send.at[j], z_recv.at[j], peer_z(offset(j)))
+
+    def first(j):
+        picks_to_scalar(j).wait()
+        for k, dest, half in ((0, at_opp, 0), (1, at_opp, 1), (2, at_right, 1), (3, at_left, 0)):
+            gather(j, k, dest, half)
+            copy_a(j, k).start()
+        for k, dest, half in ((4, at_right, 0), (5, at_left, 1), (6, a, 0), (7, a, 1)):
+            gather(j, k, dest, half)
+
+        @pl.when(j + 1 < DEPTH)
+        def _():
+            fetch(j + 1)
+
+    def second(j):
+        for k in (0, 1):
+            copy_a(j, k).wait_recv()
+            out_a[j, 4 + k] += opp_a[j, k]
+            copy_a(j, 4 + k).start()
+
+    def third(j):
+        for k in (2, 3, 4, 5):
+            copy_a(j, k).wait_recv()
+        for b_to in range(RING):
+            half, inner = b_to // 2, pl.ds(b_to % 2 * PER, PER)
+            summed = out_a[j, 6 + half, inner, :] + from_left_a[j, half, inner, :] + from_right_a[j, half, inner, :]
+            tot_a[j, b_to] = summed * parity_sign(jnp.int32(b_to), b)
+        for k in range(4):
+            copy_b(j, k).start()
+
+    def fourth(j):
+        copy_b(j, 0).wait_recv()
+        out_b[j, 0] = tot_a[j, b_right, low, :] + opp_b[j, 0]
+        copy_b(j, 4).start()
+        copy_b(j, 1).wait_recv()
+        out_b[j, 1] = tot_a[j, b_left, high, :] + opp_b[j, 1]
+        copy_b(j, 5).start()
+
+    def fifth(j):
+        for k in (2, 3, 4, 5):
+            copy_b(j, k).wait_recv()
+        sign = parity_sign(turn(z, offset(j), DEPTH), z)
+        for half, rows in ((0, low), (1, high)):
+            tot_b[j, rows, :] = (tot_a[j, b, rows, :] + from_left_b[j, half] + from_right_b[j, half]) * sign
+
+        @pl.when(j < DEPTH - 1)
+        def _():
+            copy_z(j).start()
+
+    fetch(jnp.int32(0))
+
+    def step(i, carry):
+        for late, stage in enumerate((first, second, third, fourth, fifth)):
+            j = i - LAG * late
+
+            @pl.when((j >= 0) & (j < DEPTH))
+            def _():
+                stage(j)
+
+        return carry
+
+    lax.fori_loop(0, DEPTH + 4 * LAG, step, 0)
+
+    def collect(j, rows):
+        copy_z(j).wait_recv()
+        return rows + got_z[j]
+
+    rows = lax.fori_loop(0, DEPTH - 1, collect, tot_b[DEPTH - 1])
     rows = rows * (1.0 / 1024.0)
     sketch[...] = rows
 
@@ -384,7 +394,20 @@
     gram[...] = (full_g[...] + other_g[...]) * (1.0 / (PER * 2 * RING * RING * DEPTH))
     pending = pending + [last]
 
-    for copy in [c0, c1, c2, c3, c4, c5, d0, d1, d2, d3, d4, d5] + z_copies + pending:
+    def drain(j, carry):
+        for k in range(6):
+            copy_a(j, k).wait_send()
+            copy_b(j, k).wait_send()
+
+        @pl.when(j < DEPTH - 1)
+        def _():
+            copy_z(j).wait_send()
+            picks_z(j + 1).wait_send()
+
+        return carry
+
+    lax.fori_loop(0, DEPTH, drain, 0)
+    for copy in pending:
         copy.wait_send()
 
 
@@ -422,8 +445,8 @@
 
 def shards(matrix, flips, picks):
     vmem = pl.BlockSpec(memory_space=pltpu.VMEM)
-    half_a = (PART_A, COLS)
-    half_b = (PART_B, COLS)
+    half_a = (DEPTH, 2, RING // 2 * PER, COLS)
+    half_b = (DEPTH, 2, PER // 2, COLS)
     dma = pltpu.SemaphoreType.DMA
     sketch, gram = pl.pallas_call(
         kernel,
@@ -443,15 +466,15 @@
             pltpu.VMEM((ROWS, COLS), F32),
             pltpu.VMEM((RING * RING * DEPTH, 1, PER), jnp.int32),
             pltpu.SMEM((RING * RING * DEPTH, 1, PER), jnp.int32),
-            pltpu.VMEM((6, *half_a), F32),
-            pltpu.VMEM((2, *half_a), F32),
-            pltpu.VMEM((2, *half_a), F32),
-            pltpu.VMEM((2, *half_a), F32),
-            pltpu.VMEM((2 * PART_A, COLS), F32),
-            pltpu.VMEM((2, *half_b), F32),
-            pltpu.VMEM((2, *half_b), F32),
-            pltpu.VMEM((2, *half_b), F32),
-            pltpu.VMEM((2, *half_b), F32),
+            pltpu.VMEM((DEPTH, 8, RING // 2 * PER, COLS), F32),
+            pltpu.VMEM(half_a, F32),
+            pltpu.VMEM(half_a, F32),
+            pltpu.VMEM(half_a, F32),
+            pltpu.VMEM((DEPTH, RING, PER, COLS), F32),
+            pltpu.VMEM(half_b, F32),
+            pltpu.VMEM(half_b, F32),
+            pltpu.VMEM(half_b, F32),
+            pltpu.VMEM(half_b, F32),
             pltpu.VMEM((DEPTH, PER, COLS), F32),
             pltpu.VMEM((DEPTH - 1, PER, COLS), F32),
             pltpu.VMEM((COLS, COLS), F32),
@@ -467,21 +490,21 @@
             dma((CHUNKS,)),
             dma((CHUNKS,)),
             dma((2,)),
-            dma((13,)),
-            dma((13,)),
+            dma((14,)),
+            dma((14,)),
             dma((1,)),
             dma((DEPTH,)),
-            dma((6,)),
-            dma((6,)),
-            dma((6,)),
-            dma((6,)),
+            dma((DEPTH, 6)),
+            dma((DEPTH, 6)),
+            dma((DEPTH, 6)),
+            dma((DEPTH, 6)),
             dma((7,)),
             dma((7,)),
             dma((17,)),
             dma((17,)),
         ],
         compiler_params=pltpu.CompilerParams(
-            collective_id=0, has_side_effects=True, vmem_limit_bytes=48 * 1024 * 1024
+            collective_id=0, has_side_effects=True, vmem_limit_bytes=67043328
         ),
     )(matrix, flips.reshape(ROWS // COLS, COLS), picks.reshape(1, PER))
     factor = pl.pallas_call(

time: 87 us -> 83.2 us (0.956)
  local copies, waits for them, and re-layouts: 4.18 us -> 1.37 us
  Pallas kernels: 82 us -> 81 us
    unnamed x9 -> x1, local copies, waits for them, and re-layouts: 4.18 us -> 1.37 us
    pallas_call x1, Pallas kernels: 77 us -> 76 us  [shards(): pl.pallas_call(kernel, name='blendenpik', out_shape=(jax.ShapeDtypeStruct...]
where the time goes in v3:
time: 83.2 us; the launch traced here: 83 us
  Pallas kernels  81 us (97%)
  local copies, waits for them, and re-layouts  1.37 us (2%)
    pallas_call x1, Pallas kernels, shards(): pl.pallas_call(kernel, name='blendenpik', out_shape=(jax.ShapeDtypeStruct...  76 us
    pallas_call x1, Pallas kernels, shards(): pl.pallas_call(cholesky_kernel, name='factor', out_shape=jax.ShapeDtypeSt...  5 us

profile of v3, /device:TPU:1, one launch (start us, length us, event | category | flops | bytes accessed | tf_op | source)
XLA Modules:
  0.0 83.0 jit_solution(1574672114633240757)
XLA Ops:
  0.6 76.0 %blendenpik.1 = (f32[64,128]{1,0:T(8,128)}, f32[128,128]{1,0:T(8,128)}) custom-call(f32[4096,128]{1,0:T(8,128)} %mat.1, s32[32,128]{1,0:T(8,128)} %bitcast.2, s32[1,64]{1,0:T(1,128)} %bitcast.3), custom_call_target="tpu_custom_call" | custom-call | tf_op jit(solution)/shard_map/blendenpik/pallas_call | solution.py:451
  76.6 5.0 %factor.1 = f32[128,128]{1,0:T(8,128)} custom-call(f32[128,128]{1,0:T(8,128)} %get-tuple-element.5.gram), custom_call_target="tpu_custom_call" | custom-call | tf_op jit(solution)/shard_map/factor/pallas_call | solution.py:510
  81.6 1.4 %copy.6 = f32[64,128]{1,0:T(8,128)} copy(f32[64,128]{1,0:T(8,128)} %get-tuple-element.8) | data formatting | bytes 65536

commit v4 on v3

--- a/solution.py
+++ b/solution.py
@@ -19,7 +19,8 @@
 CHUNKS = 8
 CHUNK = ROWS // CHUNKS
 LAG = 2
-PIECE = COLS // RING
+ORDER = (0, 1, 6, 4, 3, 5, 2, 7)
+PIECE = COLS // (RING * RING)
 PANEL = 16
 
 
@@ -39,12 +40,22 @@
     return (1 - 2 * (both & 1)).astype(F32).astype(BF16)
 
 
+def exact_product(rows):
+    high = rows.astype(BF16)
+    rest = rows - high.astype(F32)
+    mid = rest.astype(BF16)
+    low = (rest - mid.astype(F32)).astype(BF16)
+    first = jnp.concatenate([high, high, mid, high, low, mid], axis=0)
+    second = jnp.concatenate([high, mid, high, low, high, mid], axis=0)
+    return lax.dot_general(first, second, (((0,), (0,)), ((), ())), preferred_element_type=F32)
+
+
 def kernel(
     mat, flips_in, picks, sketch, gram,
     own, par, flips, flips_par, had, mixed, picked, picked_s,
     out_a, opp_a, from_left_a, from_right_a, tot_a,
     out_b, opp_b, from_left_b, from_right_b, tot_b,
-    got_z, part_g, got_ga, piece_b, piece_z, full_g, other_g,
+    got_z, part_g, got_g, piece_z, full_g, other_g,
     load_sem, flip_load, go, ready, core_send, core_recv, flip_sems, pick_send, pick_recv, pick_local, scalar_sem,
     a_send, a_recv, b_send, b_recv, z_send, z_recv, g_send, g_recv,
 ):
@@ -105,6 +116,45 @@
     keep = pltpu.make_async_copy(picks, picked.at[slot], pick_local.at[0])
     keep.start()
 
+    @pl.when(core == 0)
+    def _():
+        pl.semaphore_wait(barrier, 1 + len(plane))
+        signal(go.at[0], partner)
+
+    @pl.when(core == 1)
+    def _():
+        pl.semaphore_wait(go.at[0], 1)
+        for device in column:
+            signal(barrier, device)
+
+    flip_copy = remote(flips_in, flips_par, flip_sems.at[0], flip_sems.at[1], partner)
+    flip_copy.start()
+    core_copies = []
+    for k in range(CHUNKS):
+        rows = pl.ds(k * CHUNK, CHUNK)
+        copy = remote(mat.at[rows], par.at[rows], core_send.at[k], core_recv.at[k], partner)
+        copy.start()
+        core_copies.append(copy)
+
+    picks_a = [
+        remote(picks, picked.at[slot], pick_send.at[k - 1], pick_recv.at[k - 1], peer_a(k)) for k in range(1, RING)
+    ]
+
+    @pl.when(core == 0)
+    def _():
+        for copy in picks_a:
+            copy.start()
+        for device in plane:
+            signal(ready, device)
+        pl.semaphore_wait(ready, len(plane))
+        signal(go.at[1], partner)
+
+    @pl.when(core == 1)
+    def _():
+        pl.semaphore_wait(go.at[1], 1)
+        for copy in picks_a:
+            copy.start()
+
     had[...] = hadamard_block()
 
     def transformed(block, values, flip_ref, sign):
@@ -126,45 +176,6 @@
             rows = pl.ds(block * BLOCK, BLOCK)
             mixed[rows, :] = transformed(block, own[rows, :], flips, own_sign)
 
-    @pl.when(core == 0)
-    def _():
-        pl.semaphore_wait(barrier, 1 + len(plane))
-        signal(go.at[0], partner)
-
-    @pl.when(core == 1)
-    def _():
-        pl.semaphore_wait(go.at[0], 1)
-        for device in column:
-            signal(barrier, device)
-
-    flip_copy = remote(flips_in, flips_par, flip_sems.at[0], flip_sems.at[1], partner)
-    flip_copy.start()
-    core_copies = []
-    for k in range(CHUNKS):
-        rows = pl.ds(k * CHUNK, CHUNK)
-        copy = remote(mat.at[rows], par.at[rows], core_send.at[k], core_recv.at[k], partner)
-        copy.start()
-        core_copies.append(copy)
-
-    picks_a = [
-        remote(picks, picked.at[slot], pick_send.at[k - 1], pick_recv.at[k - 1], peer_a(k)) for k in range(1, RING)
-    ]
-
-    @pl.when(core == 0)
-    def _():
-        for copy in picks_a:
-            copy.start()
-        for device in plane:
-            signal(ready, device)
-        pl.semaphore_wait(ready, len(plane))
-        signal(go.at[1], partner)
-
-    @pl.when(core == 1)
-    def _():
-        pl.semaphore_wait(go.at[1], 1)
-        for copy in picks_a:
-            copy.start()
-
     def fold(k):
         core_copies[k].wait()
         for j in range(CHUNK // BLOCK):
@@ -172,6 +183,9 @@
             rows = pl.ds(block * BLOCK, BLOCK)
             mixed[rows, :] += transformed(block, par[rows, :], flips_par, par_sign)
 
+    flip_copy.wait()
+    for k in range(2):
+        fold(k)
     keep.wait()
     for copy in picks_a:
         copy.wait()
@@ -181,21 +195,20 @@
         copy = remote(picked.at[line], picked.at[line], pick_send.at[k + 2], pick_recv.at[k + 2], peer_b(k))
         copy.start()
         picks_b.append(copy)
-
-    @pl.when(core == 1)
-    def _():
-        pl.semaphore_wait(barrier, len(column))
-        signal(go.at[2], partner)
-
-    @pl.when(core == 0)
-    def _():
-        pl.semaphore_wait(go.at[2], 1)
-
-    flip_copy.wait()
-    for k in range(2):
+    for k in range(2, 6):
         fold(k)
     for copy in picks_b:
         copy.wait()
+
+    @pl.when(core == 1)
+    def _():
+        pl.semaphore_wait(barrier, len(column))
+        signal(go.at[2], partner)
+
+    @pl.when(core == 0)
+    def _():
+        pl.semaphore_wait(go.at[2], 1)
+
     layer = pl.ds(z * RING * RING, RING * RING)
 
     def picks_z(by):
@@ -204,9 +217,9 @@
             peer_z(DEPTH - by),
         )
 
-    for by in (1, 7, 2, 6, 3, 5, 4):
+    for by in (1, 6, 4, 3, 5, 2, 7):
         picks_z(by).start()
-    for k in range(2, CHUNKS):
+    for k in range(6, CHUNKS):
         fold(k)
 
     def butterfly(i, carry):
@@ -227,15 +240,17 @@
     lax.fori_loop(0, BLOCK // 8, butterfly, 0)
 
     def offset(j):
-        pair = lax.div(j, 2)
-        return (pair + 1 + lax.rem(j, 2) * (6 - 2 * pair)) * (1 - lax.div(j, DEPTH - 1))
+        place = ORDER[0]
+        for k in range(1, DEPTH):
+            place = place + (ORDER[k] - ORDER[k - 1]) * lax.div(j + DEPTH - k, DEPTH)
+        return place
 
     def picks_to_scalar(j):
         part = pl.ds(turn(z, offset(j), DEPTH) * (RING * RING), RING * RING)
         return pltpu.make_async_copy(picked.at[part], picked_s.at[part], scalar_sem.at[j])
 
     def fetch(j):
-        @pl.when(j < DEPTH - 1)
+        @pl.when(j > 0)
         def _():
             by = offset(j)
             remote(
@@ -329,7 +344,7 @@
         for half, rows in ((0, low), (1, high)):
             tot_b[j, rows, :] = (tot_a[j, b, rows, :] + from_left_b[j, half] + from_right_b[j, half]) * sign
 
-        @pl.when(j < DEPTH - 1)
+        @pl.when(j > 0)
         def _():
             copy_z(j).start()
 
@@ -351,58 +366,65 @@
         copy_z(j).wait_recv()
         return rows + got_z[j]
 
-    rows = lax.fori_loop(0, DEPTH - 1, collect, tot_b[DEPTH - 1])
+    rows = lax.fori_loop(1, DEPTH, collect, tot_b[0])
     rows = rows * (1.0 / 1024.0)
     sketch[...] = rows
 
-    part_g[...] = lax.dot_general(
-        rows, rows, (((0,), (0,)), ((), ())), precision=lax.Precision.HIGHEST, preferred_element_type=F32
-    )
+    part_g[...] = exact_product(rows)
 
     def send_g(k, src, dst, device):
         copy = remote(src, dst, g_send.at[k], g_recv.at[k], device)
         copy.start()
         return copy
 
-    def piece(position):
-        return pl.ds(pl.multiple_of(position * PIECE, PIECE), PIECE)
-
-    copies = [send_g(k - 1, part_g.at[piece(turn(a, k, RING))], got_ga.at[k - 1], peer_a(k)) for k in range(1, RING)]
+    def piece(at_a, at_b):
+        return pl.ds(pl.multiple_of((at_a * RING + at_b) * PIECE, PIECE), PIECE)
+
+    turns = [(da, db) for da in range(RING) for db in range(RING)]
+    turns.sort(key=lambda t: -min(t[0], RING - t[0]) - min(t[1], RING - t[1]))
+    pending = []
+    for da, db in turns[:-1]:
+        to_a, to_b = turn(a, da, RING), turn(b, db, RING)
+        k = da * RING + db
+        pending.append(send_g(
+            k, part_g.at[piece(to_a, to_b)], got_g.at[k], me + (to_a - a) * step_a + (to_b - b) * step_b
+        ))
+    total = part_g[piece(a, b), :]
+    for copy in pending:
+        copy.wait_recv()
+    for k in range(1, RING * RING):
+        total = total + got_g[k]
+    piece_z[z] = total
+    copies = [send_g(15 + k, piece_z.at[z], piece_z.at[z], peer_z(k)) for k in (4, 3, 5, 2, 6, 1, 7)]
     for copy in copies:
         copy.wait_recv()
-    piece_b[b] = part_g[piece(a), :] + got_ga[0] + got_ga[1] + got_ga[2]
-    pending = copies
-    copies = [send_g(k + 2, piece_b.at[b], piece_b.at[b], peer_b(k)) for k in range(1, RING)]
-    for copy in copies:
-        copy.wait_recv()
-    piece_z[z] = piece_b[0] + piece_b[1] + piece_b[2] + piece_b[3]
     pending = pending + copies
-    copies = [send_g(k + 5, piece_z.at[z], piece_z.at[z], peer_z(k)) for k in (4, 3, 5, 2, 6, 1, 7)]
-    for copy in copies:
-        copy.wait_recv()
     total = piece_z[0]
     for k in range(1, DEPTH):
         total = total + piece_z[k]
-    full_g[piece(a), :] = total
-    pending = pending + copies
-    copies = [send_g(k + 12, full_g.at[piece(a)], full_g.at[piece(a)], peer_a(k)) for k in range(1, RING)]
+    full_g[piece(a, b), :] = total
+    mine = full_g.at[piece(a, b)]
+    copies = []
+    for da, db in turns:
+        k = da * RING + db
+        there = me + (turn(a, da, RING) - a) * step_a + (turn(b, db, RING) - b) * step_b
+        copies.append(send_g(38 + k, mine, other_g.at[piece(a, b)], there + 1 - 2 * core))
+        if k:
+            copies.append(send_g(22 + k, mine, mine, there))
     for copy in copies:
         copy.wait_recv()
     pending = pending + copies
-    last = send_g(16, full_g, other_g, partner)
-    last.wait_recv()
     gram[...] = (full_g[...] + other_g[...]) * (1.0 / (PER * 2 * RING * RING * DEPTH))
-    pending = pending + [last]
 
     def drain(j, carry):
         for k in range(6):
             copy_a(j, k).wait_send()
             copy_b(j, k).wait_send()
 
-        @pl.when(j < DEPTH - 1)
+        @pl.when(j > 0)
         def _():
             copy_z(j).wait_send()
-            picks_z(j + 1).wait_send()
+            picks_z(j).wait_send()
 
         return carry
 
@@ -411,10 +433,15 @@
         copy.wait_send()
 
 
-def cholesky_kernel(gram, factor, work, upper):
+def cholesky_kernel(gram, sketch_in, factor, sketch, work, upper, rows, sems):
+    fetch = pltpu.make_async_copy(sketch_in, rows, sems.at[0])
+    fetch.start()
     work[...] = gram[...]
     row = lax.broadcasted_iota(jnp.int32, (PANEL, COLS), 0)
     lane = lax.broadcasted_iota(jnp.int32, (PANEL, COLS), 1)
+    fetch.wait()
+    store = pltpu.make_async_copy(rows, sketch, sems.at[1])
+    store.start()
     for base in range(0, COLS, PANEL):
         panel = work[pl.ds(base, PANEL), :]
         columns = [jnp.broadcast_to(panel[:, base + k : base + k + 1], (PANEL, COLS)) for k in range(PANEL)]
@@ -431,16 +458,11 @@
         scaled = jnp.where(lane >= base + row, panel * root, 0.0)
         upper[pl.ds(base, PANEL), :] = scaled
         if base + PANEL < COLS:
-            high = scaled.astype(BF16)
-            rest = scaled - high.astype(F32)
-            mid = rest.astype(BF16)
-            low = (rest - mid.astype(F32)).astype(BF16)
-            first = jnp.concatenate([high, high, mid, high, low, mid], axis=0)
-            second = jnp.concatenate([high, mid, high, low, high, mid], axis=0)
-            update = lax.dot_general(first, second, (((0,), (0,)), ((), ())), preferred_element_type=F32)
+            update = exact_product(scaled)
             after = base + PANEL
             work[pl.ds(after, COLS - after), :] -= update[after:, :]
     factor[...] = upper[...].T
+    store.wait()
 
 
 def shards(matrix, flips, picks):
@@ -476,10 +498,9 @@
             pltpu.VMEM(half_b, F32),
             pltpu.VMEM(half_b, F32),
             pltpu.VMEM((DEPTH, PER, COLS), F32),
-            pltpu.VMEM((DEPTH - 1, PER, COLS), F32),
+            pltpu.VMEM((DEPTH, PER, COLS), F32),
             pltpu.VMEM((COLS, COLS), F32),
-            pltpu.VMEM((RING - 1, PIECE, COLS), F32),
-            pltpu.VMEM((RING, PIECE, COLS), F32),
+            pltpu.VMEM((RING * RING, PIECE, COLS), F32),
             pltpu.VMEM((DEPTH, PIECE, COLS), F32),
             pltpu.VMEM((COLS, COLS), F32),
             pltpu.VMEM((COLS, COLS), F32),
@@ -498,23 +519,29 @@
             dma((DEPTH, 6)),
             dma((DEPTH, 6)),
             dma((DEPTH, 6)),
-            dma((7,)),
-            dma((7,)),
-            dma((17,)),
-            dma((17,)),
+            dma((DEPTH,)),
+            dma((DEPTH,)),
+            dma((54,)),
+            dma((54,)),
         ],
         compiler_params=pltpu.CompilerParams(
             collective_id=0, has_side_effects=True, vmem_limit_bytes=67043328
         ),
     )(matrix, flips.reshape(ROWS // COLS, COLS), picks.reshape(1, PER))
-    factor = pl.pallas_call(
+    hbm = pl.BlockSpec(memory_space=pltpu.HBM)
+    factor, sketch = pl.pallas_call(
         cholesky_kernel,
         name="factor",
-        out_shape=jax.ShapeDtypeStruct((COLS, COLS), F32),
-        in_specs=[vmem],
-        out_specs=vmem,
-        scratch_shapes=[pltpu.VMEM((COLS, COLS), F32)] * 2,
-    )(gram)
+        out_shape=(jax.ShapeDtypeStruct((COLS, COLS), F32), jax.ShapeDtypeStruct((PER, COLS), F32)),
+        in_specs=[vmem, hbm],
+        out_specs=(vmem, hbm),
+        scratch_shapes=[
+            pltpu.VMEM((COLS, COLS), F32),
+            pltpu.VMEM((COLS, COLS), F32),
+            pltpu.VMEM((PER, COLS), F32),
+            dma((2,)),
+        ],
+    )(gram, sketch)
     return (sketch, factor)
 
 

time: 83.2 us -> 77.4 us (0.930)
  Pallas kernels: 81 us -> 76.5 us
  local copies, waits for them, and re-layouts: 1.37 us -> 0 us
    pallas_call x1, Pallas kernels: 76 us -> 70.8 us  [shards(): pl.pallas_call(kernel, name='blendenpik', out_shape=(jax.ShapeDtypeStruct...]
    unnamed x1 -> x0, local copies, waits for them, and re-layouts: 1.37 us -> none
where the time goes in v4:
time: 77.4 us; the launch traced here: 77.2 us
  Pallas kernels  76.5 us (99%)
    pallas_call x1, Pallas kernels, shards(): pl.pallas_call(kernel, name='blendenpik', out_shape=(jax.ShapeDtypeStruct...  70.8 us
    pallas_call x1, Pallas kernels, shards(): pl.pallas_call(cholesky_kernel, name='factor', out_shape=(jax.ShapeDtypeS...  5.77 us

profile of v4, /device:TPU:1, one launch (start us, length us, event | category | flops | bytes accessed | tf_op | source)
XLA Modules:
  0.0 77.2 jit_solution(5973362798777156866)
XLA Ops:
  0.6 70.8 %blendenpik.1 = (f32[64,128]{1,0:T(8,128)}, f32[128,128]{1,0:T(8,128)}) custom-call(f32[4096,128]{1,0:T(8,128)} %mat.1, s32[32,128]{1,0:T(8,128)} %bitcast.2, s32[1,64]{1,0:T(1,128)} %bitcast.3), custom_call_target="tpu_custom_call" | custom-call | tf_op jit(solution)/shard_map/blendenpik/pallas_call | solution.py:473
  71.4 5.8 %factor.1 = (f32[128,128]{1,0:T(8,128)}, f32[64,128]{1,0:T(8,128)}) custom-call(f32[128,128]{1,0:T(8,128)} %get-tuple-element.6.gram, f32[64,128]{1,0:T(8,128)} %get-tuple-element.7.sketch_in), custom_call_target="tpu_custom_call" | custom-call | tf_op jit(solution)/shard_map/factor/pallas_call | solution.py:532

commit v5 on v4

--- a/solution.py
+++ b/solution.py
@@ -19,7 +19,7 @@
 CHUNKS = 8
 CHUNK = ROWS // CHUNKS
 LAG = 2
-ORDER = (0, 1, 6, 4, 3, 5, 2, 7)
+ORDER = (0, 4, 5, 3, 6, 2, 7, 1)
 PIECE = COLS // (RING * RING)
 PANEL = 16
 
@@ -54,8 +54,7 @@
     mat, flips_in, picks, sketch, gram,
     own, par, flips, flips_par, had, mixed, picked, picked_s,
     out_a, opp_a, from_left_a, from_right_a, tot_a,
-    out_b, opp_b, from_left_b, from_right_b, tot_b,
-    got_z, part_g, got_g, piece_z, full_g, other_g,
+    got_z, tot_z, got_b, part_g, got_g, piece_z, full_g, other_g,
     load_sem, flip_load, go, ready, core_send, core_recv, flip_sems, pick_send, pick_recv, pick_local, scalar_sem,
     a_send, a_recv, b_send, b_recv, z_send, z_recv, g_send, g_recv,
 ):
@@ -146,14 +145,6 @@
             copy.start()
         for device in plane:
             signal(ready, device)
-        pl.semaphore_wait(ready, len(plane))
-        signal(go.at[1], partner)
-
-    @pl.when(core == 1)
-    def _():
-        pl.semaphore_wait(go.at[1], 1)
-        for copy in picks_a:
-            copy.start()
 
     had[...] = hadamard_block()
 
@@ -175,6 +166,19 @@
             block = k * (CHUNK // BLOCK) + j
             rows = pl.ds(block * BLOCK, BLOCK)
             mixed[rows, :] = transformed(block, own[rows, :], flips, own_sign)
+        if k == 2:
+
+            @pl.when(core == 0)
+            def _():
+                pl.semaphore_wait(ready, len(plane))
+                signal(go.at[1], partner)
+
+            @pl.when(core == 1)
+            def _():
+                pl.semaphore_wait(go.at[1], 1)
+                for copy in picks_a:
+                    copy.start()
+
 
     def fold(k):
         core_copies[k].wait()
@@ -183,9 +187,6 @@
             rows = pl.ds(block * BLOCK, BLOCK)
             mixed[rows, :] += transformed(block, par[rows, :], flips_par, par_sign)
 
-    flip_copy.wait()
-    for k in range(2):
-        fold(k)
     keep.wait()
     for copy in picks_a:
         copy.wait()
@@ -195,7 +196,8 @@
         copy = remote(picked.at[line], picked.at[line], pick_send.at[k + 2], pick_recv.at[k + 2], peer_b(k))
         copy.start()
         picks_b.append(copy)
-    for k in range(2, 6):
+    flip_copy.wait()
+    for k in range(3):
         fold(k)
     for copy in picks_b:
         copy.wait()
@@ -217,9 +219,9 @@
             peer_z(DEPTH - by),
         )
 
-    for by in (1, 6, 4, 3, 5, 2, 7):
+    for by in (4, 5, 3, 6, 2, 7, 1):
         picks_z(by).start()
-    for k in range(6, CHUNKS):
+    for k in range(3, CHUNKS):
         fold(k)
 
     def butterfly(i, carry):
@@ -275,8 +277,6 @@
 
     right, left = peer_a(1), peer_a(RING - 1)
     at_right, at_left, at_opp = turn(a, 1, RING), turn(a, 3, RING), turn(a, 2, RING)
-    b_right, b_left, b_opp = turn(b, 1, RING), turn(b, 3, RING), turn(b, 2, RING)
-    right_b, left_b = peer_b(1), peer_b(RING - 1)
 
     def copy_a(j, k):
         dst = (
@@ -285,21 +285,9 @@
         )[k]
         return remote(out_a.at[j, k], dst, a_send.at[j, k], a_recv.at[j, k], left if k % 2 else right)
 
-    low, high = pl.ds(0, PER // 2), pl.ds(PER // 2, PER // 2)
-
-    def copy_b(j, k):
-        src, dst = (
-            (tot_a.at[j, b_opp, low], opp_b.at[j, 0]),
-            (tot_a.at[j, b_opp, high], opp_b.at[j, 1]),
-            (tot_a.at[j, b_right, high], from_left_b.at[j, 1]),
-            (tot_a.at[j, b_left, low], from_right_b.at[j, 0]),
-            (out_b.at[j, 0], from_left_b.at[j, 0]),
-            (out_b.at[j, 1], from_right_b.at[j, 1]),
-        )[k]
-        return remote(src, dst, b_send.at[j, k], b_recv.at[j, k], left_b if k % 2 else right_b)
-
     def copy_z(j):
-        return remote(tot_b.at[j], got_z.at[j], z_send.at[j], z_recv.at[j], peer_z(offset(j)))
+        ahead = turn(z, 1 + (DEPTH - 2) * (1 - lax.rem(j, 2)), DEPTH)
+        return remote(tot_a.at[j], got_z.at[j], z_send.at[j], z_recv.at[j], me + (ahead - z) * (2 * RING * RING))
 
     def first(j):
         picks_to_scalar(j).wait()
@@ -322,27 +310,17 @@
     def third(j):
         for k in (2, 3, 4, 5):
             copy_a(j, k).wait_recv()
+        sign = parity_sign(turn(z, offset(j), DEPTH), z)
         for b_to in range(RING):
             half, inner = b_to // 2, pl.ds(b_to % 2 * PER, PER)
             summed = out_a[j, 6 + half, inner, :] + from_left_a[j, half, inner, :] + from_right_a[j, half, inner, :]
-            tot_a[j, b_to] = summed * parity_sign(jnp.int32(b_to), b)
-        for k in range(4):
-            copy_b(j, k).start()
-
-    def fourth(j):
-        copy_b(j, 0).wait_recv()
-        out_b[j, 0] = tot_a[j, b_right, low, :] + opp_b[j, 0]
-        copy_b(j, 4).start()
-        copy_b(j, 1).wait_recv()
-        out_b[j, 1] = tot_a[j, b_left, high, :] + opp_b[j, 1]
-        copy_b(j, 5).start()
-
-    def fifth(j):
-        for k in (2, 3, 4, 5):
-            copy_b(j, k).wait_recv()
-        sign = parity_sign(turn(z, offset(j), DEPTH), z)
-        for half, rows in ((0, low), (1, high)):
-            tot_b[j, rows, :] = (tot_a[j, b, rows, :] + from_left_b[j, half] + from_right_b[j, half]) * sign
+            tot_a[j, b_to] = summed * sign
+
+        @pl.when(j > 2)
+        def _():
+            copy_z(j - 2).wait_recv()
+            for b_to in range(RING):
+                tot_a[j, b_to] += got_z[j - 2, b_to]
 
         @pl.when(j > 0)
         def _():
@@ -351,7 +329,7 @@
     fetch(jnp.int32(0))
 
     def step(i, carry):
-        for late, stage in enumerate((first, second, third, fourth, fifth)):
+        for late, stage in enumerate((first, second, third)):
             j = i - LAG * late
 
             @pl.when((j >= 0) & (j < DEPTH))
@@ -360,13 +338,24 @@
 
         return carry
 
-    lax.fori_loop(0, DEPTH + 4 * LAG, step, 0)
-
-    def collect(j, rows):
-        copy_z(j).wait_recv()
-        return rows + got_z[j]
-
-    rows = lax.fori_loop(1, DEPTH, collect, tot_b[0])
+    lax.fori_loop(0, DEPTH + 2 * LAG, step, 0)
+
+    for j in (DEPTH - 2, DEPTH - 1):
+        copy_z(jnp.int32(j)).wait_recv()
+    for b_to in range(RING):
+        summed = tot_a[0, b_to] + got_z[DEPTH - 2, b_to] + got_z[DEPTH - 1, b_to]
+        tot_z[b_to] = summed * parity_sign(jnp.int32(b_to), b)
+
+    b_copies = []
+    for k in (2, 1, 3):
+        copy = remote(
+            tot_z.at[turn(b, k, RING)], got_b.at[k - 1], b_send.at[k - 1], b_recv.at[k - 1], peer_b(k)
+        )
+        copy.start()
+        b_copies.append(copy)
+    for copy in b_copies:
+        copy.wait_recv()
+    rows = tot_z[b] + got_b[0] + got_b[1] + got_b[2]
     rows = rows * (1.0 / 1024.0)
     sketch[...] = rows
 
@@ -389,6 +378,20 @@
         pending.append(send_g(
             k, part_g.at[piece(to_a, to_b)], got_g.at[k], me + (to_a - a) * step_a + (to_b - b) * step_b
         ))
+    def drain(j, carry):
+        for k in range(6):
+            copy_a(j, k).wait_send()
+
+        @pl.when(j > 0)
+        def _():
+            copy_z(j).wait_send()
+            picks_z(j).wait_send()
+
+        return carry
+
+    lax.fori_loop(0, DEPTH, drain, 0)
+    for copy in b_copies:
+        copy.wait_send()
     total = part_g[piece(a, b), :]
     for copy in pending:
         copy.wait_recv()
@@ -411,25 +414,13 @@
         copies.append(send_g(38 + k, mine, other_g.at[piece(a, b)], there + 1 - 2 * core))
         if k:
             copies.append(send_g(22 + k, mine, mine, there))
+    for copy in pending:
+        copy.wait_send()
     for copy in copies:
         copy.wait_recv()
-    pending = pending + copies
     gram[...] = (full_g[...] + other_g[...]) * (1.0 / (PER * 2 * RING * RING * DEPTH))
 
-    def drain(j, carry):
-        for k in range(6):
-            copy_a(j, k).wait_send()
-            copy_b(j, k).wait_send()
-
-        @pl.when(j > 0)
-        def _():
-            copy_z(j).wait_send()
-            picks_z(j).wait_send()
-
-        return carry
-
-    lax.fori_loop(0, DEPTH, drain, 0)
-    for copy in pending:
+    for copy in copies:
         copy.wait_send()
 
 
@@ -468,7 +459,6 @@
 def shards(matrix, flips, picks):
     vmem = pl.BlockSpec(memory_space=pltpu.VMEM)
     half_a = (DEPTH, 2, RING // 2 * PER, COLS)
-    half_b = (DEPTH, 2, PER // 2, COLS)
     dma = pltpu.SemaphoreType.DMA
     sketch, gram = pl.pallas_call(
         kernel,
@@ -493,12 +483,9 @@
             pltpu.VMEM(half_a, F32),
             pltpu.VMEM(half_a, F32),
             pltpu.VMEM((DEPTH, RING, PER, COLS), F32),
-            pltpu.VMEM(half_b, F32),
-            pltpu.VMEM(half_b, F32),
-            pltpu.VMEM(half_b, F32),
-            pltpu.VMEM(half_b, F32),
-            pltpu.VMEM((DEPTH, PER, COLS), F32),
-            pltpu.VMEM((DEPTH, PER, COLS), F32),
+            pltpu.VMEM((DEPTH, RING, PER, COLS), F32),
+            pltpu.VMEM((RING, PER, COLS), F32),
+            pltpu.VMEM((RING - 1, PER, COLS), F32),
             pltpu.VMEM((COLS, COLS), F32),
             pltpu.VMEM((RING * RING, PIECE, COLS), F32),
             pltpu.VMEM((DEPTH, PIECE, COLS), F32),
@@ -517,8 +504,8 @@
             dma((DEPTH,)),
             dma((DEPTH, 6)),
             dma((DEPTH, 6)),
-            dma((DEPTH, 6)),
-            dma((DEPTH, 6)),
+            dma((3,)),
+            dma((3,)),
             dma((DEPTH,)),
             dma((DEPTH,)),
             dma((54,)),

time: 77.4 us -> 77.1 us (level)
  no operation moved by 1% of the time
where the time goes in v5:
time: 77.1 us; the launch traced here: 76.9 us
  Pallas kernels  76.2 us (99%)
    pallas_call x1, Pallas kernels, shards(): pl.pallas_call(kernel, name='blendenpik', out_shape=(jax.ShapeDtypeStruct...  70.4 us
    pallas_call x1, Pallas kernels, shards(): pl.pallas_call(cholesky_kernel, name='factor', out_shape=(jax.ShapeDtypeS...  5.77 us

profile of v5, /device:TPU:1, one launch (start us, length us, event | category | flops | bytes accessed | tf_op | source)
XLA Modules:
  0.0 76.9 jit_solution(2957479056979584842)
XLA Ops:
  0.6 70.4 %blendenpik.1 = (f32[64,128]{1,0:T(8,128)}, f32[128,128]{1,0:T(8,128)}) custom-call(f32[4096,128]{1,0:T(8,128)} %mat.1, s32[32,128]{1,0:T(8,128)} %bitcast.2, s32[1,64]{1,0:T(1,128)} %bitcast.3), custom_call_target="tpu_custom_call" | custom-call | tf_op jit(solution)/shard_map/blendenpik/pallas_call | solution.py:463
  71.1 5.8 %factor.1 = (f32[128,128]{1,0:T(8,128)}, f32[64,128]{1,0:T(8,128)}) custom-call(f32[128,128]{1,0:T(8,128)} %get-tuple-element.6.gram, f32[64,128]{1,0:T(8,128)} %get-tuple-element.7.sketch_in), custom_call_target="tpu_custom_call" | custom-call | tf_op jit(solution)/shard_map/factor/pallas_call | solution.py:519

commit v6 on v5

--- a/solution.py
+++ b/solution.py
@@ -18,7 +18,6 @@
 BLOCKS = ROWS // BLOCK
 CHUNKS = 8
 CHUNK = ROWS // CHUNKS
-LAG = 2
 ORDER = (0, 4, 5, 3, 6, 2, 7, 1)
 PIECE = COLS // (RING * RING)
 PANEL = 16
@@ -290,6 +289,10 @@
         return remote(tot_a.at[j], got_z.at[j], z_send.at[j], z_recv.at[j], me + (ahead - z) * (2 * RING * RING))
 
     def first(j):
+        @pl.when(j == 1)
+        def _():
+            fetch(j)
+
         picks_to_scalar(j).wait()
         for k, dest, half in ((0, at_opp, 0), (1, at_opp, 1), (2, at_right, 1), (3, at_left, 0)):
             gather(j, k, dest, half)
@@ -297,7 +300,7 @@
         for k, dest, half in ((4, at_right, 0), (5, at_left, 1), (6, a, 0), (7, a, 1)):
             gather(j, k, dest, half)
 
-        @pl.when(j + 1 < DEPTH)
+        @pl.when((j > 0) & (j + 1 < DEPTH))
         def _():
             fetch(j + 1)
 
@@ -329,8 +332,8 @@
     fetch(jnp.int32(0))
 
     def step(i, carry):
-        for late, stage in enumerate((first, second, third)):
-            j = i - LAG * late
+        for late, stage in ((1, second), (0, first), (3, third)):
+            j = i - late
 
             @pl.when((j >= 0) & (j < DEPTH))
             def _():
@@ -338,7 +341,7 @@
 
         return carry
 
-    lax.fori_loop(0, DEPTH + 2 * LAG, step, 0)
+    lax.fori_loop(0, DEPTH + 3, step, 0)
 
     for j in (DEPTH - 2, DEPTH - 1):
         copy_z(jnp.int32(j)).wait_recv()

time: 77.1 us -> 89.6 us (1.16)
  Pallas kernels: 76.2 us -> 88.7 us
    pallas_call x1, Pallas kernels: 70.4 us -> 82.9 us  [shards(): pl.pallas_call(kernel, name='blendenpik', out_shape=(jax.ShapeDtypeStruct...]
where the time goes in v6:
time: 89.6 us; the launch traced here: 89.3 us
  Pallas kernels  88.7 us (99%)
    pallas_call x1, Pallas kernels, shards(): pl.pallas_call(kernel, name='blendenpik', out_shape=(jax.ShapeDtypeStruct...  82.9 us
    pallas_call x1, Pallas kernels, shards(): pl.pallas_call(cholesky_kernel, name='factor', out_shape=(jax.ShapeDtypeS...  5.77 us

profile of v6, /device:TPU:1, one launch (start us, length us, event | category | flops | bytes accessed | tf_op | source)
XLA Modules:
  0.0 89.3 jit_solution(6906105802515735367)
XLA Ops:
  0.6 82.9 %blendenpik.1 = (f32[64,128]{1,0:T(8,128)}, f32[128,128]{1,0:T(8,128)}) custom-call(f32[4096,128]{1,0:T(8,128)} %mat.1, s32[32,128]{1,0:T(8,128)} %bitcast.2, s32[1,64]{1,0:T(1,128)} %bitcast.3), custom_call_target="tpu_custom_call" | custom-call | tf_op jit(solution)/shard_map/blendenpik/pallas_call | solution.py:466
  83.6 5.8 %factor.1 = (f32[128,128]{1,0:T(8,128)}, f32[64,128]{1,0:T(8,128)}) custom-call(f32[128,128]{1,0:T(8,128)} %get-tuple-element.6.gram, f32[64,128]{1,0:T(8,128)} %get-tuple-element.7.sketch_in), custom_call_target="tpu_custom_call" | custom-call | tf_op jit(solution)/shard_map/factor/pallas_call | solution.py:522
